TPU v7x, 512 devices: a whole 4x4x16 slice. The times are simulated.
512 devices in a mesh: lvl: 16 (over z), col: 32 (over y, x, core).
Axes of the slice: x: 4, y: 4, z: 16, core: 2. Of those that a mesh axis runs over, the one named last changes fastest.
Arguments:
- rhs: float32 [16, 1536, 128], P('lvl', 'col'), may hold values from -6 to 6
- panel: bfloat16 [16, 4, 1536, 1536], P('lvl', None, 'col'), may hold values from -0.078125 to 0.078125
- inverse_t: bfloat16 [16, 1536, 1536], P('lvl', 'col'), as said below
- pattern: int32 [16, 4, 12, 12], P('lvl'), may hold values 0 or 1
Outputs:
- sample: float32 [16, 1536, 128], P('lvl', 'col')
- solution: float32 [16, 1536, 128], P('lvl', 'col')
Inputs may be any that keep to these rules, and one draw needn't show every extreme that they name: `pattern`: 1 marks a 128 x 128 tile of a panel slot that is structurally nonzero. Each inverse_t[s] is upper triangular with a positive diagonal.
All inputs are finite; a program needn't handle non-finite values.
Results may differ from a plain program's by a relative error of at most 0.035.
Values may be sent and summed in bfloat16 or wider, within the bound.
A program may use at most 64 MiB of HBM per device.

v0:
```python
import jax
import jax.numpy as jnp
from jax import lax
from jax.sharding import PartitionSpec as P


def as_sent(x):

    def short(part):
        return part.astype(jnp.bfloat16) if part.dtype == jnp.float32 else part

    return jax.tree.map(short, x)


def level_rank(device_pos, levels):
    running = jnp.zeros((), jnp.int32)
    for exponent in range(1, levels + 1):
        running = running + ((device_pos + 1) % 2**exponent == 0).astype(jnp.int32)
    return running


def expand_pattern(pattern_own, row_start, row_count, full_width):
    tile_count = pattern_own.shape[1]
    tile_size = full_width // tile_count
    row_ids = row_start + lax.iota(jnp.int32, row_count)
    row_pick = (row_ids[:, None] // tile_size == lax.iota(jnp.int32, tile_count)[None, :]).astype(
        jnp.bfloat16
    )
    col_pick = (
        lax.iota(jnp.int32, full_width)[None, :] // tile_size
        == lax.iota(jnp.int32, tile_count)[:, None]
    ).astype(jnp.bfloat16)
    row_mask = jnp.einsum(
        "rb,kbc->krc",
        row_pick,
        pattern_own.astype(jnp.bfloat16),
        preferred_element_type=jnp.float32,
    ).astype(jnp.bfloat16)
    return jnp.einsum("krc,cn->krn", row_mask, col_pick, preferred_element_type=jnp.float32).astype(
        jnp.bfloat16
    )


def pick_member(everyone, member_pos, member_total):
    safe_pos = jnp.clip(member_pos, 0, member_total - 1)
    picked = lax.dynamic_index_in_dim(everyone, safe_pos, 0, keepdims=False)
    inside = jnp.logical_and(member_pos >= 0, member_pos < member_total)
    return jnp.where(inside, picked, jnp.zeros_like(picked))


def on_device(rhs, panel, inverse_t, pattern):
    member_total = lax.axis_size("lvl")
    levels = member_total.bit_length() - 1
    device_pos = lax.axis_index("lvl")
    column_pos = lax.axis_index("col")
    row_count = rhs.shape[1]
    rhs_count = rhs.shape[2]
    full_width = inverse_t.shape[2]
    height = level_rank(device_pos, levels)
    right_side = rhs[0]
    inverse_own = inverse_t[0]
    factor = panel[0] * expand_pattern(pattern[0], column_pos * row_count, row_count, full_width)
    sample = jnp.zeros((row_count, rhs_count), jnp.float32)
    upward = jnp.zeros((levels + 1, row_count, rhs_count), jnp.float32)
    for section_num in range(levels + 1):
        if section_num == 0:
            gathered = upward
        else:
            reach_dist = 2 ** (section_num - 1)
            everyone = lax.all_gather(as_sent(upward[None]), "lvl", axis=0, tiled=True)
            from_left = pick_member(everyone, device_pos - reach_dist, member_total)
            from_right = pick_member(everyone, device_pos + reach_dist, member_total)
            gathered = from_left + from_right
        active = height == section_num
        residual = (right_side - gathered[0]).astype(jnp.bfloat16)
        partial_sum = jnp.einsum(
            "ri,rn->in", inverse_own, residual, preferred_element_type=jnp.float32
        )
        solved_all = lax.psum(partial_sum.astype(jnp.bfloat16), "col").astype(jnp.float32)
        own_rows = lax.dynamic_slice_in_dim(solved_all, column_pos * row_count, row_count, 0)
        solved_half = solved_all.astype(jnp.bfloat16)
        sample = jnp.where(active, own_rows, sample)
        remain = levels - section_num
        if remain > 0:
            pushed = jnp.einsum(
                "krn,nm->krm", factor[:remain], solved_half, preferred_element_type=jnp.float32
            )
            upward = jnp.where(active, pushed + gathered[1 : remain + 1], 0.0)
    answer = jnp.zeros((row_count, rhs_count), jnp.float32)
    ancestry = jnp.zeros((levels, row_count, rhs_count), jnp.bfloat16)
    downward = ancestry
    for section_num in range(levels, -1, -1):
        remain = levels - section_num
        active = height == section_num
        if remain > 0:
            reach_dist = 2**section_num
            everyone = lax.all_gather(downward[None], "lvl", axis=0, tiled=True)
            parent_up = device_pos // (2 * reach_dist) % 2 == 0
            parent_pos = jnp.where(parent_up, device_pos + reach_dist, device_pos - reach_dist)
            received = pick_member(everyone, parent_pos, member_total)
            ancestry = ancestry.at[:remain].set(jnp.where(active, received, ancestry[:remain]))
            partial_adj = jnp.einsum(
                "krn,krm->nm",
                factor[:remain],
                ancestry[:remain],
                preferred_element_type=jnp.float32,
            )
            adjoint = lax.psum_scatter(
                partial_adj.astype(jnp.bfloat16), "col", scatter_dimension=0, tiled=True
            ).astype(jnp.float32)
            back_full = sample - adjoint
        else:
            back_full = sample
        back_whole = lax.all_gather(back_full.astype(jnp.bfloat16), "col", axis=0, tiled=True)
        solved = jnp.dot(inverse_own, back_whole, preferred_element_type=jnp.float32)
        answer = jnp.where(active, solved, answer)
        solved_half = solved.astype(jnp.bfloat16)
        if section_num > 0:
            downward = jnp.concatenate(
                [solved_half[None], ancestry[: levels - section_num]], axis=0
            )
    return (sample[None], answer[None])


def solution(mesh):
    in_specs = (
        P("lvl", "col", None),
        P("lvl", None, "col", None),
        P("lvl", "col", None),
        P("lvl", None, None, None),
    )
    out_specs = (P("lvl", "col", None), P("lvl", "col", None))
    return jax.shard_map(
        on_device, mesh=mesh, in_specs=in_specs, out_specs=out_specs, check_vma=False
    )
```

profile of v0, /device:TPU:1, one launch (start us, length us, event | category | flops | bytes accessed | tf_op | source)
XLA Modules:
  0.0 1450.9 jit_solution(16410489634673471)
XLA Ops:
  7.2 0.0 all-reduce.7.cloned.1.call-start
  7.2 0.8 copy-done
  8.1 1.8 convolution_convert_fusion.6
  9.9 0.0 all-reduce.7.cloned.1.call-update
  9.9 0.0 all-reduce.9.cloned.1.call-start
  10.1 0.6 fusion
  10.7 139.2 %all-reduce.7.cloned.1.call-done = bf16[1536,128]{1,0:T(8,128)(2,1)} async-done(((bf16[1536,128]{1,0:T(8,128)(2,1)}), bf16[1536,128]{1,0:T(8,128)(2,1)}) %all-reduce.7.cloned.1.call-update) | async-done | bytes 393232 | tf_op jit(solution)/shard_map/psum | solution.py:79
  149.9 1.3 fusion.8
  151.2 28.1 %all-gather = bf16[64,48,128]{2,1,0:T(8,128)(2,1)S(1)} all-gather(bf16[4,48,128]{2,1,0:T(8,128)(2,1)S(1)} %fusion.8), channel_id=2, replica_groups=mesh['lvl'=16,'col'=32] {'lvl'}, dimensions={0}, use_global_device_ids=true | all-gather | bytes 835584 | tf_op jit(solution)/shard_map/all_gather | solution.py:70
  179.3 1.1 fusion.4
  180.4 0.0 all-reduce.9.cloned.1.call-update
  180.5 0.0 all-reduce.11.cloned.1.call-start
  180.5 136.0 %all-reduce.9.cloned.1.call-done = bf16[1536,128]{1,0:T(8,128)(2,1)} async-done(((bf16[1536,128]{1,0:T(8,128)(2,1)}), bf16[1536,128]{1,0:T(8,128)(2,1)}) %all-reduce.9.cloned.1.call-update) | async-done | bytes 393232 | tf_op jit(solution)/shard_map/psum | solution.py:79
  316.5 1.3 fusion.10
  317.8 27.0 %all-gather.1 = bf16[48,48,128]{2,1,0:T(8,128)(2,1)S(1)} all-gather(bf16[3,48,128]{2,1,0:T(8,128)(2,1)S(1)} %fusion.10), channel_id=3, replica_groups=mesh['lvl'=16,'col'=32] {'lvl'}, dimensions={0}, use_global_device_ids=true | all-gather | bytes 626688 | tf_op jit(solution)/shard_map/all_gather | solution.py:70
  344.8 1.1 fusion.5
  345.9 0.0 all-reduce.11.cloned.1.call-update
  345.9 0.0 all-reduce.13.cloned.1.call-start
  346.0 135.6 %all-reduce.11.cloned.1.call-done = bf16[1536,128]{1,0:T(8,128)(2,1)} async-done(((bf16[1536,128]{1,0:T(8,128)(2,1)}), bf16[1536,128]{1,0:T(8,128)(2,1)}) %all-reduce.11.cloned.1.call-update) | async-done | bytes 393232 | tf_op jit(solution)/shard_map/psum | solution.py:79
  481.6 1.2 fusion.12
  482.8 26.0 %all-gather.2 = bf16[32,48,128]{2,1,0:T(8,128)(2,1)S(1)} all-gather(bf16[2,48,128]{2,1,0:T(8,128)(2,1)S(1)} %fusion.12), channel_id=4, replica_groups=mesh['lvl'=16,'col'=32] {'lvl'}, dimensions={0}, use_global_device_ids=true | all-gather | bytes 417792 | tf_op jit(solution)/shard_map/all_gather | solution.py:70
  508.8 1.1 fusion.6
  509.9 0.0 all-reduce.13.cloned.1.call-update
  509.9 0.0 all-reduce.15.cloned.1.call-start
  510.0 135.7 %all-reduce.13.cloned.1.call-done = bf16[1536,128]{1,0:T(8,128)(2,1)} async-done(((bf16[1536,128]{1,0:T(8,128)(2,1)}), bf16[1536,128]{1,0:T(8,128)(2,1)}) %all-reduce.13.cloned.1.call-update) | async-done | bytes 393232 | tf_op jit(solution)/shard_map/psum | solution.py:79
  645.7 1.2 fusion.16
  646.9 24.3 %all-gather.3 = bf16[16,48,128]{2,1,0:T(8,128)(2,1)S(1)} all-gather(bf16[1,48,128]{2,1,0:T(8,128)(2,1)S(1)} %fusion.16), channel_id=5, replica_groups=mesh['lvl'=16,'col'=32] {'lvl'}, dimensions={0}, use_global_device_ids=true | all-gather | bytes 208896 | tf_op jit(solution)/shard_map/all_gather | solution.py:70
  671.2 1.1 fusion.7
  672.3 0.0 all-reduce.15.cloned.1.call-update
  672.3 0.0 reduce-scatter.5.cloned.1.call-start
  672.4 136.2 %all-reduce.15.cloned.1.call-done = bf16[1536,128]{1,0:T(8,128)(2,1)} async-done(((bf16[1536,128]{1,0:T(8,128)(2,1)}), bf16[1536,128]{1,0:T(8,128)(2,1)}) %all-reduce.15.cloned.1.call-update) | async-done | bytes 393232 | tf_op jit(solution)/shard_map/psum | solution.py:79
  808.6 0.8 fusion.84
  809.4 25.8 %all_gather.43 = bf16[1536,128]{1,0:T(8,128)(2,1)S(1)} all-gather(bf16[48,128]{1,0:T(8,128)(2,1)S(1)} %get-tuple-element.62), channel_id=1, replica_groups=mesh['lvl'=16,'col'=32] {'col'}, dimensions={0}, use_global_device_ids=true | all-gather | bytes 405504 | tf_op jit(solution)/shard_map/all_gather | solution.py:114
  835.3 0.2 fusion.21
  835.5 24.6 %all-gather.4 = bf16[768,128]{1,0:T(8,128)(2,1)S(1)} all-gather(bf16[48,128]{1,0:T(8,128)(2,1)S(1)} %convert_bitcast_fusion.3), channel_id=6, replica_groups=mesh['lvl'=16,'col'=32] {'lvl'}, dimensions={0}, use_global_device_ids=true | all-gather | bytes 208896 | tf_op jit(solution)/shard_map/all_gather | solution.py:97
  860.2 1.1 convolution_convert_fusion.1
  861.2 0.0 reduce-scatter.5.cloned.1.call-update
  861.2 0.0 reduce-scatter.7.cloned.1.call-start
  861.4 96.8 %reduce-scatter.5.cloned.1.call-done = bf16[48,128]{1,0:T(8,128)(2,1)} async-done(((bf16[1536,128]{1,0:T(8,128)(2,1)}), bf16[48,128]{1,0:T(8,128)(2,1)}) %reduce-scatter.5.cloned.1.call-update) | async-done | bytes 12304 | tf_op jit(solution)/shard_map/reduce_scatter | solution.py:108
  958.1 0.7 subtract_convert_fusion.3
  958.8 26.6 %all_gather.45 = bf16[1536,128]{1,0:T(8,128)(2,1)S(1)} all-gather(bf16[48,128]{1,0:T(8,128)(2,1)S(1)} %subtract_convert_fusion.3), channel_id=1, replica_groups=mesh['lvl'=16,'col'=32] {'col'}, dimensions={0}, use_global_device_ids=true | all-gather | bytes 405504 | tf_op jit(solution)/shard_map/all_gather | solution.py:114
  985.4 0.2 fusion.23
  985.6 25.8 %all-gather.5 = bf16[32,48,128]{2,1,0:T(8,128)(2,1)S(1)} all-gather(bf16[2,48,128]{2,1,0:T(8,128)(2,1)S(1)} %pad_maximum_fusion.2), channel_id=7, replica_groups=mesh['lvl'=16,'col'=32] {'lvl'}, dimensions={0}, use_global_device_ids=true | all-gather | bytes 417792 | tf_op jit(solution)/shard_map/all_gather | solution.py:97
  1011.4 1.0 fusion.2
  1012.4 0.0 reduce-scatter.7.cloned.1.call-update
  1012.5 0.0 reduce-scatter.9.cloned.1.call-start
  1012.5 97.4 %reduce-scatter.7.cloned.1.call-done = bf16[48,128]{1,0:T(8,128)(2,1)} async-done(((bf16[1536,128]{1,0:T(8,128)(2,1)}), bf16[48,128]{1,0:T(8,128)(2,1)}) %reduce-scatter.7.cloned.1.call-update) | async-done | bytes 12304 | tf_op jit(solution)/shard_map/reduce_scatter | solution.py:108
  1110.0 0.7 subtract_convert_fusion.2
  1110.7 26.3 %all_gather.47 = bf16[1536,128]{1,0:T(8,128)(2,1)S(1)} all-gather(bf16[48,128]{1,0:T(8,128)(2,1)S(1)} %subtract_convert_fusion.2), channel_id=1, replica_groups=mesh['lvl'=16,'col'=32] {'col'}, dimensions={0}, use_global_device_ids=true | all-gather | bytes 405504 | tf_op jit(solution)/shard_map/all_gather | solution.py:114
  1137.0 0.2 fusion.25
  1137.2 26.6 %all-gather.6 = bf16[48,48,128]{2,1,0:T(8,128)(2,1)S(1)} all-gather(bf16[3,48,128]{2,1,0:T(8,128)(2,1)S(1)} %pad_maximum_fusion.1), channel_id=8, replica_groups=mesh['lvl'=16,'col'=32] {'lvl'}, dimensions={0}, use_global_device_ids=true | all-gather | bytes 626688 | tf_op jit(solution)/shard_map/all_gather | solution.py:97
  1163.9 1.2 fusion.3
  1165.0 0.0 reduce-scatter.11.cloned.1.call-start
  1165.1 97.6 %reduce-scatter.9.cloned.1.call-done = bf16[48,128]{1,0:T(8,128)(2,1)} async-done(((bf16[1536,128]{1,0:T(8,128)(2,1)}), bf16[48,128]{1,0:T(8,128)(2,1)}) %reduce-scatter.9.cloned.1.call-update) | async-done | bytes 12304 | tf_op jit(solution)/shard_map/reduce_scatter | solution.py:108
  1262.7 0.7 subtract_convert_fusion.1
  1263.4 26.3 %all_gather.49 = bf16[1536,128]{1,0:T(8,128)(2,1)S(1)} all-gather(bf16[48,128]{1,0:T(8,128)(2,1)S(1)} %subtract_convert_fusion.1), channel_id=1, replica_groups=mesh['lvl'=16,'col'=32] {'col'}, dimensions={0}, use_global_device_ids=true | all-gather | bytes 405504 | tf_op jit(solution)/shard_map/all_gather | solution.py:114
  1289.7 0.2 fusion.27
  1289.9 27.8 %all-gather.7 = bf16[64,48,128]{2,1,0:T(8,128)(2,1)S(1)} all-gather(bf16[4,48,128]{2,1,0:T(8,128)(2,1)S(1)} %pad_maximum_fusion), channel_id=9, replica_groups=mesh['lvl'=16,'col'=32] {'lvl'}, dimensions={0}, use_global_device_ids=true | all-gather | bytes 835584 | tf_op jit(solution)/shard_map/all_gather | solution.py:97
  1317.7 1.2 fusion.1
  1318.8 0.0 reduce-scatter.11.cloned.1.call-update
  1318.9 97.7 %reduce-scatter.11.cloned.1.call-done = bf16[48,128]{1,0:T(8,128)(2,1)} async-done(((bf16[1536,128]{1,0:T(8,128)(2,1)}), bf16[48,128]{1,0:T(8,128)(2,1)}) %reduce-scatter.11.cloned.1.call-update) | async-done | bytes 12304 | tf_op jit(solution)/shard_map/reduce_scatter | solution.py:108
  1416.6 0.7 subtract_convert_fusion
  1417.3 26.3 %all_gather.51 = bf16[1536,128]{1,0:T(8,128)(2,1)S(1)} all-gather(bf16[48,128]{1,0:T(8,128)(2,1)S(1)} %subtract_convert_fusion), channel_id=1, replica_groups=mesh['lvl'=16,'col'=32] {'col'}, dimensions={0}, use_global_device_ids=true | all-gather | bytes 405504 | tf_op jit(solution)/shard_map/all_gather | solution.py:114
  1443.5 0.8 fusion.13
  (27 shorter events, 0.2 us)
Async XLA Ops:
  7.2 0.9 copy-start
  7.2 2.9 copy-start.4
  7.2 2.9 copy-start.3
  7.2 142.7 %all-reduce.7.cloned.1.call-start = ((), (), s32[]{:S(2)}) async-start(), calls=%async_computation.4 | async-start | bytes 786432 | tf_op jit(solution)/shard_map/psum | solution.py:79
  9.9 306.6 %all-reduce.9.cloned.1.call-start = ((), (), s32[]{:S(2)}) async-start(), calls=%async_computation.5 | async-start | bytes 786432 | tf_op jit(solution)/shard_map/psum | solution.py:79
  10.7 168.6 %copy-start.1 = (f32[1,48,128]{2,1,0:T(8,128)S(1)}, f32[1,48,128]{2,1,0:T(8,128)}, u32[]{:S(2)}) copy-start(f32[1,48,128]{2,1,0:T(8,128)} %param.14) | copy-start | bytes 73732
  180.5 301.1 %all-reduce.11.cloned.1.call-start = ((), (), s32[]{:S(2)}) async-start(), calls=%async_computation.6 | async-start | bytes 786432 | tf_op jit(solution)/shard_map/psum | solution.py:79
  345.9 299.8 %all-reduce.13.cloned.1.call-start = ((), (), s32[]{:S(2)}) async-start(), calls=%async_computation.7 | async-start | bytes 786432 | tf_op jit(solution)/shard_map/psum | solution.py:79
  509.9 298.7 %all-reduce.15.cloned.1.call-start = ((), (), s32[]{:S(2)}) async-start(), calls=%async_computation.8 | async-start | bytes 786432 | tf_op jit(solution)/shard_map/psum | solution.py:79
  672.3 285.8 %reduce-scatter.5.cloned.1.call-start = ((), (), s32[]{:S(2)}) async-start(), calls=%async_computation.9 | async-start | bytes 405504 | tf_op jit(solution)/shard_map/reduce_scatter | solution.py:108
  809.4 607.1 %copy-start.2 = (f32[48,128]{1,0:T(8,128)}, f32[48,128]{1,0:T(8,128)S(1)}, u32[]{:S(2)}) copy-start(f32[48,128]{1,0:T(8,128)S(1)} %get-tuple-element.63) | copy-start | bytes 73732
  861.2 248.8 %reduce-scatter.7.cloned.1.call-start = ((), (), s32[]{:S(2)}) async-start(), calls=%async_computation.10 | async-start | bytes 405504 | tf_op jit(solution)/shard_map/reduce_scatter | solution.py:108
  1012.5 250.2 %reduce-scatter.9.cloned.1.call-start = ((), (), s32[]{:S(2)}) async-start(), calls=%async_computation.11 | async-start | bytes 405504 | tf_op jit(solution)/shard_map/reduce_scatter | solution.py:108
  1165.0 251.5 %reduce-scatter.11.cloned.1.call-start = ((), (), s32[]{:S(2)}) async-start(), calls=%async_computation.12 | async-start | bytes 405504 | tf_op jit(solution)/shard_map/reduce_scatter | solution.py:108
Sparse Core Ops, SparseCore 0:
  11.2 138.5 all-reduce.6
  180.6 135.8 all-reduce.8
  346.0 135.5 all-reduce.10
  510.0 135.6 all-reduce.12
  672.4 136.1 all-reduce.14
  861.3 96.7 reduce-scatter.4
  1012.6 97.3 reduce-scatter.6
  1165.2 97.4 reduce-scatter.8
  1319.0 97.5 reduce-scatter.10
where the time goes:
time: 1450 us
  waiting for transfers between devices  1070 us (74%)
  blocking collectives  341 us (24%)
  matrix products  17.7 us (1%)
    psum x5, waiting for transfers between devices, on_device(): lax.psum(partial_sum.astype(jnp.bfloat16), 'col').astype(jnp.float32)  683 us
    reduce_scatter x4, waiting for transfers between devices, on_device(): lax.psum_scatter(partial_adj.astype(jnp.bfloat16), 'col', scatter_dimensi...  389 us
    all_gather x5, blocking collectives, on_device(): lax.all_gather(back_full.astype(jnp.bfloat16), 'col', axis=0, tiled=True)  131 us
    all_gather x4, blocking collectives, on_device(): everyone = lax.all_gather(as_sent(upward[None]), 'lvl', axis=0, tiled=True)  105 us
    all_gather x4, blocking collectives, on_device(): everyone = lax.all_gather(downward[None], 'lvl', axis=0, tiled=True)  105 us
  transfers between devices with their start and end apart: 9, of which 9 were waited for; matrix products, arithmetic and copies ran while one was open for 0% of the time, Pallas kernels for 0%

commit v1 on v0

v1 whole, which is shorter than its diff:
```python
import functools

import jax
import jax.numpy as jnp
from jax import lax
from jax.experimental import pallas as pl
from jax.experimental.pallas import tpu as pltpu
from jax.sharding import PartitionSpec as P

MESH = pl.DeviceIdType.MESH
NT = (((1,), (1,)), ((), ()))
NX = 4
NY = 4
NV = 2 * NX


def remote(src, dst, send_sem, recv_sem, lvl, col):
    return pltpu.make_async_remote_copy(
        src_ref=src,
        dst_ref=dst,
        send_sem=send_sem,
        recv_sem=recv_sem,
        device_id=(lvl, col),
        device_id_type=MESH,
    )


def arrived(dst, sem):
    pltpu.make_async_copy(dst, dst, sem).wait()


def kernel(
    nodes,
    rhs_ref,
    panel_ref,
    inverse_ref,
    pattern_ref,
    sample_ref,
    answer_ref,
    factor,
    inv,
    turned,
    rhs_in,
    rhs_all,
    first_in,
    later_in,
    push,
    sample_t,
    total,
    piece_out,
    sample_in,
    parent_in,
    above,
    part_out,
    own_in,
    solved_out,
    solved_in,
    gx_send,
    gx_recv,
    gy_send,
    gy_recv,
    rhs_send,
    rhs_recv,
    row_send,
    row_recv,
    up0_send,
    up0_recv,
    up_send,
    up_recv,
    down0_send,
    down0_recv,
    down_send,
    down_recv,
    own_send,
    own_recv,
    sample_send,
    sample_recv,
    solved_send,
    solved_recv,
):
    rows = rhs_ref.shape[0]
    width = inv.shape[1]
    slots = panel_ref.shape[0]
    tiles = pattern_ref.shape[2]
    tile = width // tiles
    span = NV * rows
    half = span // 2
    few = rhs_ref.shape[1] // NV

    s = lax.axis_index("lvl")
    c = lax.axis_index("col")
    y, v = c // NV, c % NV
    x, core = v // 2, v % 2
    other = 1 - core
    xp, xm, xo = (x + 1) % NX, (x + 3) % NX, (x + 2) % NX
    yp, ym, yo = (y + 1) % NY, (y + 3) % NY, (y + 2) % NY

    level = 0
    step = 1
    for e in range(1, slots + 1):
        whole = 1 - ((s + 1) % 2**e + 2**e - 1) // 2**e
        level = level + whole
        step = step + whole * 2 ** (e - 1)
    side = (s // (2 * step)) % 2
    parent = (s + step * (1 - 2 * side)) % nodes
    left = (s + nodes - step // 2) % nodes
    right = (s + step // 2) % nodes
    is_root = s == nodes - 1
    has_parent = s != nodes - 1
    has_left = s % 2 == 1
    has_right = jnp.logical_and(s % 2 == 1, s != nodes - 1)
    not_root = 1 - (s + 1) // nodes
    inner = s % 2

    def chip(yy, xx, cc):
        return (yy * NX + xx) * 2 + cc

    def mult(value, by):
        return pl.multiple_of(value, by)

    own_span = pl.ds(mult(y * span, 128), span)

    barrier = pltpu.get_barrier_semaphore()

    def greet(lvl, col):
        pl.semaphore_signal(barrier, inc=1, device_id=(lvl, col), device_id_type=MESH)

    for d in range(1, NV):
        greet(s, y * NV + (v + d) % NV)
    for d in range(1, NY):
        greet(s, (y + d) % NY * NV + v)

    @pl.when(has_parent)
    def _():
        for w in range(NY):
            greet(parent, w * NV + v)

    @pl.when(has_left)
    def _():
        for w in range(NY):
            greet(left, w * NV + v)

    @pl.when(has_right)
    def _():
        for w in range(NY):
            greet(right, w * NV + v)

    own_rows = pl.ds(mult(v * rows, 16), rows)
    inv[pl.ds(mult(c * rows, 16), rows), :] = inverse_ref[...]
    piece = 16

    def mask_slot(k):
        for q in range(rows // piece):
            tile_row = (c * rows + q * piece) // tile
            for j in range(tiles):
                keep = pattern_ref[k, tile_row, j].astype(jnp.float32)
                block = panel_ref[k, q * piece : (q + 1) * piece, j * tile : (j + 1) * tile]
                kept = (block.astype(jnp.float32) * keep).astype(jnp.bfloat16)
                factor[
                    k,
                    pl.ds(mult(v * rows + q * piece, 16), piece),
                    j * tile : (j + 1) * tile,
                ] = kept

    mask_slot(0)
    padded = jnp.concatenate(
        [rhs_ref[...], jnp.zeros((128 - rows, rhs_ref.shape[1]), jnp.float32)], axis=0
    )
    turned[...] = padded.T.reshape(NV, few, 128)
    rhs_in[v] = turned[v]

    @pl.when(s % 2 == 0)
    def _():
        first_in[0] = jnp.zeros_like(first_in[0])
        later_in[...] = jnp.zeros_like(later_in)

    @pl.when(jnp.logical_or(s % 2 == 0, is_root))
    def _():
        first_in[1] = jnp.zeros_like(first_in[1])

    pl.semaphore_wait(barrier, NV - 1 + NY - 1 + NY * (not_root + inner + inner * not_root))

    def block(g, xx, cc, lo, hi):
        if g == 0:
            start = mult(y * span + (2 * xx + cc) * rows, 16)
            return inv.at[pl.ds(start, rows), lo:hi]
        return factor.at[g - 1, pl.ds(mult((2 * xx + cc) * rows, 16), rows), lo:hi]

    mid = width // 2

    def gx_copy(g, i):
        ref, col = (
            lambda: (block(g, x, core, 0, width), chip(y, xp, core)),
            lambda: (block(g, x, core, 0, width), chip(y, xm, core)),
            lambda: (block(g, xm, core, 0, mid), chip(y, xp, core)),
            lambda: (block(g, xp, core, mid, width), chip(y, xm, core)),
            lambda: (block(g, x, core, 0, width), chip(y, x, other)),
            lambda: (block(g, xm, core, 0, width), chip(y, x, other)),
            lambda: (block(g, xp, core, 0, width), chip(y, x, other)),
            lambda: (block(g, xo, core, 0, width), chip(y, x, other)),
        )[i]()
        return remote(ref, ref, gx_send.at[g, i], gx_recv.at[g, i], s, col)

    def gx_wait(g, i):
        ref = (
            lambda: block(g, xm, core, 0, width),
            lambda: block(g, xp, core, 0, width),
            lambda: block(g, xo, core, 0, mid),
            lambda: block(g, xo, core, mid, width),
            lambda: block(g, x, other, 0, width),
            lambda: block(g, xm, other, 0, width),
            lambda: block(g, xp, other, 0, width),
            lambda: block(g, xo, other, 0, width),
        )[i]()
        arrived(ref, gx_recv.at[g, i])

    def gx_start(g):
        for i in (0, 1, 4):
            gx_copy(g, i).start()

    def gx_relay(g):
        gx_wait(g, 0)
        gx_copy(g, 2).start()
        gx_copy(g, 5).start()
        gx_wait(g, 1)
        gx_copy(g, 3).start()
        gx_copy(g, 6).start()

    def gx_last(g):
        gx_wait(g, 2)
        gx_wait(g, 3)
        gx_copy(g, 7).start()

    def gx_finish(g):
        for i in (4, 5, 6, 7):
            gx_wait(g, i)

    def stripe(yy, cc, lo, hi):
        return inv.at[pl.ds(mult(yy * span + cc * half + lo, 16), hi - lo), :]

    cut = half // 2

    def gy_copy(i):
        ref, col = (
            lambda: (stripe(y, core, 0, half), chip(yp, x, core)),
            lambda: (stripe(y, core, 0, half), chip(ym, x, core)),
            lambda: (stripe(ym, core, 0, cut), chip(yp, x, core)),
            lambda: (stripe(yp, core, cut, half), chip(ym, x, core)),
            lambda: (stripe(ym, core, 0, half), chip(y, x, other)),
            lambda: (stripe(yp, core, 0, half), chip(y, x, other)),
            lambda: (stripe(yo, core, 0, half), chip(y, x, other)),
        )[i]()
        return remote(ref, ref, gy_send.at[i], gy_recv.at[i], s, col)

    def gy_wait(i):
        ref = (
            lambda: stripe(ym, core, 0, half),
            lambda: stripe(yp, core, 0, half),
            lambda: stripe(yo, core, 0, cut),
            lambda: stripe(yo, core, cut, half),
            lambda: stripe(ym, other, 0, half),
            lambda: stripe(yp, other, 0, half),
            lambda: stripe(yo, other, 0, half),
        )[i]()
        arrived(ref, gy_recv.at[i])

    def rhs_copy(d):
        to = (v + d) % NV
        return remote(turned.at[to], rhs_in.at[v], rhs_send.at[d], rhs_recv.at[d], s, y * NV + to)

    def row_copy(d):
        ref = rhs_all.at[:, own_span]
        return remote(ref, ref, row_send.at[d], row_recv.at[d], s, (y + d) % NY * NV + v)

    gx_start(0)
    for d in range(1, NV):
        rhs_copy(d).start()
    gx_start(1)
    for k in range(1, slots):
        mask_slot(k)
    gx_relay(0)
    gx_last(0)
    gx_finish(0)
    gy_copy(0).start()
    gy_copy(1).start()

    for d in range(1, NV):
        arrived(rhs_in.at[(v + NV - d) % NV], rhs_recv.at[d])
    lane = lax.broadcasted_iota(jnp.int32, (few, 128), 1)
    joined = [jnp.zeros((few, 128), jnp.float32) for _ in range(span // 128)]
    for q in range(NV):
        a, b = divmod(q * rows, 128)
        moved = pltpu.roll(rhs_in[q], b, axis=1) if b else rhs_in[q]
        if b + rows <= 128:
            joined[a] = joined[a] + moved
        else:
            joined[a] = joined[a] + jnp.where(lane >= b, moved, 0.0)
            joined[a + 1] = joined[a + 1] + jnp.where(lane >= b, 0.0, moved)
    rhs_all[:, own_span] = jnp.concatenate(joined, axis=1)
    for d in range(1, NY):
        row_copy(d).start()

    gx_relay(1)
    gx_last(1)
    if slots > 1:
        gx_start(2)
    gx_finish(1)
    gy_wait(0)
    gy_copy(2).start()
    gy_copy(4).start()
    gy_wait(1)
    gy_copy(3).start()
    gy_copy(5).start()
    if slots > 1:
        gx_relay(2)
        gx_last(2)
        if slots > 2:
            gx_start(3)
    gy_wait(2)
    gy_wait(3)
    gy_copy(6).start()
    for d in range(1, NY):
        arrived(
            rhs_all.at[:, pl.ds(mult((y + NY - d) % NY * span, 128), span)], row_recv.at[d]
        )
    for i in (4, 5, 6):
        gy_wait(i)

    def up0_copy(w):
        return remote(
            push.at[0],
            first_in.at[side, :, own_span],
            up0_send.at[w],
            up0_recv.at[side, y],
            parent,
            w * NV + v,
        )

    def up_copy(k):
        return remote(
            push.at[k],
            later_in.at[side, k - 1],
            up_send.at[k],
            up_recv.at[side, k - 1],
            parent,
            y * NV + v,
        )

    @pl.when(has_left)
    def _():
        for w in range(NY):
            arrived(first_in.at[0, :, w * span : (w + 1) * span], up0_recv.at[0, w])

    @pl.when(has_right)
    def _():
        for w in range(NY):
            arrived(first_in.at[1, :, w * span : (w + 1) * span], up0_recv.at[1, w])

    incoming = first_in[0].astype(jnp.float32) + first_in[1].astype(jnp.float32)
    residual = (rhs_all[...] - incoming).astype(jnp.bfloat16)
    for w in range(NY):
        to = (w + 1) * span
        sample_t[:, w * span : to] = jnp.dot(
            residual[:, :to], inv[:to, w * span : to], preferred_element_type=jnp.float32
        )
    sample_half = sample_t[...].astype(jnp.bfloat16)

    def pushed(k):
        out = lax.dot_general(sample_half, factor[k], NT, preferred_element_type=jnp.float32)
        if k < slots - 1:

            @pl.when(has_left)
            def _():
                for i in range(2):
                    arrived(later_in.at[i, k], up_recv.at[i, k])

            out = out + later_in[0, k].astype(jnp.float32) + later_in[1, k].astype(jnp.float32)
        push[k] = out.astype(jnp.bfloat16)

    @pl.when(has_parent)
    def _():
        pushed(0)
        for w in range(NY):
            up0_copy(w).start()

    for k in range(1, slots):
        if k > 1:
            gx_relay(k + 1)
            gx_last(k + 1)
            if k + 2 <= slots:
                gx_start(k + 2)
        gx_finish(k + 1)

        @pl.when(level + k < slots)
        def _():
            pushed(k)
            up_copy(k).start()

    def cut_pieces(ref, value):
        parts = [value[:, 128 * a : 128 * (a + 1)] for a in range(span // 128)]
        for q in range(NV):
            a, b = divmod(q * rows, 128)
            moved = pltpu.roll(parts[a], 128 - b, axis=1) if b else parts[a]
            if b + rows > 128:
                after = pltpu.roll(parts[a + 1], 128 - b, axis=1)
                moved = jnp.where(lane < 128 - b, moved, after)
            ref[q] = moved

    def sample_copy(d):
        to = (v + d) % NV
        return remote(
            piece_out.at[to], sample_in.at[v], sample_send.at[d], sample_recv.at[d], s, y * NV + to
        )

    def solved_copy(d):
        to = (v + d) % NV
        return remote(
            solved_out.at[to], solved_in.at[v], solved_send.at[d], solved_recv.at[d], s, y * NV + to
        )

    cut_pieces(piece_out, sample_t[:, own_span])
    sample_in[v] = piece_out[v]
    for d in range(1, NV):
        sample_copy(d).start()

    def down_copy(k, child, i):
        return remote(
            above.at[k],
            above.at[k + 1],
            down_send.at[i, k],
            down_recv.at[k + 1],
            child,
            y * NV + v,
        )

    def down0_copy(w, child, i):
        return remote(
            part_out.at[w],
            parent_in.at[y],
            down0_send.at[i, w],
            down0_recv.at[y],
            child,
            w * NV + v,
        )

    def own_copy(d):
        to = (y + d) % NY
        return remote(part_out.at[to], own_in.at[y], own_send.at[d], own_recv.at[d], s, to * NV + v)

    def hand_down(k):
        @pl.when(has_left)
        def _():
            down_copy(k, left, 0).start()

        @pl.when(has_right)
        def _():
            down_copy(k, right, 1).start()

    group = lax.broadcasted_iota(jnp.int32, (few, width), 1) // span
    total[...] = jnp.where(group == y, sample_t[...], 0.0)
    for k in range(slots - 1, 0, -1):

        @pl.when(level + k < slots)
        def _():
            arrived(above.at[k], down_recv.at[k])
            if k < slots - 1:
                hand_down(k)
            total[...] -= jnp.dot(above[k], factor[k], preferred_element_type=jnp.float32)

    @pl.when(has_parent)
    def _():
        for w in range(NY):
            arrived(parent_in.at[w], down0_recv.at[w])
        summed = parent_in[0].astype(jnp.float32)
        for w in range(1, NY):
            summed = summed + parent_in[w].astype(jnp.float32)
        above[0] = summed.astype(jnp.bfloat16)
        total[...] -= jnp.dot(above[0], factor[0], preferred_element_type=jnp.float32)

    back = total[...].astype(jnp.bfloat16)
    for w in range(NY):
        start = w * span
        part = lax.dot_general(
            back[:, start:],
            inv[start : start + span, start:],
            NT,
            preferred_element_type=jnp.float32,
        )
        part_out[w] = part.astype(jnp.bfloat16)

        @pl.when(has_left)
        def _():
            down0_copy(w, left, 0).start()

        @pl.when(has_right)
        def _():
            down0_copy(w, right, 1).start()

    own_in[y] = part_out[y]
    for d in range(1, NY):
        own_copy(d).start()

    @pl.when(has_parent)
    def _():
        if slots > 1:
            hand_down(0)

    for d in range(1, NV):
        arrived(sample_in.at[(v + NV - d) % NV], sample_recv.at[d])
    sample_ref[...] = sample_in[...].reshape(NV * few, 128).T[:rows, :]

    for d in range(1, NY):
        arrived(own_in.at[(y + NY - d) % NY], own_recv.at[d])
    solved = own_in[0].astype(jnp.float32)
    for w in range(1, NY):
        solved = solved + own_in[w].astype(jnp.float32)
    cut_pieces(solved_out, solved)
    solved_in[v] = solved_out[v]
    for d in range(1, NV):
        solved_copy(d).start()
    for d in range(1, NV):
        arrived(solved_in.at[(v + NV - d) % NV], solved_recv.at[d])
    answer_ref[...] = solved_in[...].reshape(NV * few, 128).T[:rows, :]

    for g in range(slots + 1):
        for i in range(8):
            gx_copy(g, i).wait_send()
    for i in range(7):
        gy_copy(i).wait_send()
    for d in range(1, NV):
        rhs_copy(d).wait_send()
        sample_copy(d).wait_send()
        solved_copy(d).wait_send()
    for d in range(1, NY):
        row_copy(d).wait_send()
        own_copy(d).wait_send()

    @pl.when(has_parent)
    def _():
        for w in range(NY):
            up0_copy(w).wait_send()

    for k in range(1, slots):

        @pl.when(level + k < slots)
        def _():
            up_copy(k).wait_send()

    for i, (cond, child) in enumerate(((has_left, left), (has_right, right))):

        @pl.when(cond)
        def _():
            for w in range(NY):
                down0_copy(w, child, i).wait_send()

        for k in range(slots - 1):

            @pl.when(jnp.logical_and(cond, level + k < slots))
            def _():
                down_copy(k, child, i).wait_send()


def on_device(nodes, rhs, panel, inverse_t, pattern):
    rows, count = rhs.shape[1:]
    slots = panel.shape[1]
    width = inverse_t.shape[2]
    span = NV * rows
    few = count // NV
    f32, bf16 = jnp.float32, jnp.bfloat16
    dma = pltpu.SemaphoreType.DMA
    vmem = pl.BlockSpec(memory_space=pltpu.VMEM)
    outs = pl.pallas_call(
        functools.partial(kernel, nodes),
        out_shape=[jax.ShapeDtypeStruct((rows, count), f32)] * 2,
        in_specs=[vmem, vmem, vmem, pl.BlockSpec(memory_space=pltpu.SMEM)],
        out_specs=[vmem, vmem],
        scratch_shapes=[
            pltpu.VMEM((slots, span, width), bf16),
            pltpu.VMEM((width, width), bf16),
            pltpu.VMEM((NV, few, 128), f32),
            pltpu.VMEM((NV, few, 128), f32),
            pltpu.VMEM((few, width), f32),
            pltpu.VMEM((2, few, width), bf16),
            pltpu.VMEM((2, max(slots - 1, 1), few, span), bf16),
            pltpu.VMEM((slots, few, span), bf16),
            pltpu.VMEM((few, width), f32),
            pltpu.VMEM((few, width), f32),
            pltpu.VMEM((NV, few, 128), f32),
            pltpu.VMEM((NV, few, 128), f32),
            pltpu.VMEM((NY, few, span), bf16),
            pltpu.VMEM((slots, few, span), bf16),
            pltpu.VMEM((NY, few, span), bf16),
            pltpu.VMEM((NY, few, span), bf16),
            pltpu.VMEM((NV, few, 128), f32),
            pltpu.VMEM((NV, few, 128), f32),
        ]
        + [dma((slots + 1, 8))] * 2
        + [dma((7,))] * 2
        + [dma((NV,))] * 2
        + [dma((NY,))] * 2
        + [dma((NY,)), dma((2, NY))]
        + [dma((slots,)), dma((2, slots))]
        + [dma((2, NY)), dma((NY,))]
        + [dma((2, slots)), dma((slots,))]
        + [dma((NY,))] * 2
        + [dma((NV,))] * 4,
        compiler_params=pltpu.CompilerParams(
            collective_id=0, has_side_effects=True, vmem_limit_bytes=40 * 2**20
        ),
    )(rhs[0], panel[0], inverse_t[0], pattern[0])
    return outs[0][None], outs[1][None]


def solution(mesh):
    in_specs = (
        P("lvl", "col", None),
        P("lvl", None, "col", None),
        P("lvl", "col", None),
        P("lvl", None, None, None),
    )
    out_specs = (P("lvl", "col", None), P("lvl", "col", None))
    return jax.shard_map(
        functools.partial(on_device, mesh.shape["lvl"]),
        mesh=mesh,
        in_specs=in_specs,
        out_specs=out_specs,
        check_vma=False,
    )
```

time: 1450 us -> 148 us (0.10)
  waiting for transfers between devices: 1070 us -> 0 us
  blocking collectives: 341 us -> 0 us
  Pallas kernels: 0 us -> 143 us
  matrix products: 17.7 us -> 0 us
    psum x5 -> x0, waiting for transfers between devices: 683 us -> none  [on_device(): lax.psum(partial_sum.astype(jnp.bfloat16), 'col').astype(jnp.float32)]
    reduce_scatter x4 -> x0, waiting for transfers between devices: 389 us -> none  [on_device(): lax.psum_scatter(partial_adj.astype(jnp.bfloat16), 'col', scatter_dimensi...]
    all_gather x13 -> x0, blocking collectives: 341 us -> none  [the longest x5 131 us: on_device(): lax.all_gather(back_full.astype(jnp.bfloat16), 'col', axis=0, tiled=True)]
    pallas_call x0 -> x1, Pallas kernels: none -> 143 us  [on_device(): pl.pallas_call(functools.partial(kernel, nodes), out_shape=[jax.ShapeDtyp...]
    dot_general x19 -> x0, matrix products: 17.7 us -> none  [the longest x5 6.13 us: on_device(): jnp.einsum('ri,rn->in', inverse_own, residual, preferred_element_type=jnp...]
  transfers between devices with their start and end apart: 9 -> 0, of which waited for: 9 -> 0; matrix products, arithmetic and copies ran while one was open for 0% -> 0% of each run, Pallas kernels for 0% -> 0%
where the time goes in v1:
time: 148 us; the launch traced here: 147 us
  Pallas kernels  143 us (97%)
  local copies, waits for them, and re-layouts  3.94 us (3%)
    pallas_call x1, Pallas kernels, on_device(): pl.pallas_call(functools.partial(kernel, nodes), out_shape=[jax.ShapeDtyp...  143 us
    unnamed x9, local copies, waits for them, and re-layouts  3.94 us

profile of v1, /device:TPU:1, one launch (start us, length us, event | category | flops | bytes accessed | tf_op | source)
XLA Modules:
  0.0 147.3 jit_solution(14099159140570026214)
XLA Ops:
  0.6 0.0 copy-start.2
  0.6 0.7 copy.8
  1.4 0.0 copy-done.2
  1.4 0.0 copy-start
  1.4 1.1 copy-done
  2.5 0.0 copy-start.1
  2.5 0.9 copy-done.1
  3.4 142.7 %shard_map.59 = (f32[48,128]{1,0:T(8,128)S(1)}, f32[48,128]{1,0:T(8,128)S(1)}) custom-call(f32[48,128]{1,0:T(8,128)S(1)} %bitcast.11, bf16[4,48,1536]{2,1,0:T(8,128)(2,1)S(1)} %bitcast.8, bf16[48,1536]{1,0:T(8,128)(2,1)S(1)} %bitcast.9, s32[4,12,12]{2,1,0:T(8,128)S(1)} %bitcast.10), custom_call_target="tpu_custom_call" | custom-call | tf_op jit(solution)/shard_map/pallas_call | solution.py:572
  146.1 0.6 copy.11
  146.7 0.6 copy.12
Async XLA Ops:
  0.6 0.8 copy-start.2
  1.4 1.1 copy-start
  2.5 0.9 copy-start.1

commit v2 on v1

v2 whole, which is shorter than its diff:
```python
import functools

import jax
import jax.numpy as jnp
from jax import lax
from jax.experimental import pallas as pl
from jax.experimental.pallas import tpu as pltpu
from jax.sharding import PartitionSpec as P

MESH = pl.DeviceIdType.MESH
NT = (((1,), (1,)), ((), ()))
NX = 4
NY = 4
NV = 2 * NX
ORDER = (1, 3, 2)


def remote(src, dst, send_sem, recv_sem, lvl, col):
    return pltpu.make_async_remote_copy(
        src_ref=src,
        dst_ref=dst,
        send_sem=send_sem,
        recv_sem=recv_sem,
        device_id=(lvl, col),
        device_id_type=MESH,
    )


def arrived(dst, sem):
    pltpu.make_async_copy(dst, dst, sem).wait()


def kernel(
    nodes,
    rhs_ref,
    panel_ref,
    inverse_ref,
    pattern_ref,
    sample_ref,
    answer_ref,
    factor,
    inv,
    top_inv,
    turned,
    rhs_in,
    rhs_all,
    top_rhs,
    first_in,
    later_in,
    push,
    shares,
    sample_t,
    total,
    piece_out,
    sample_in,
    parent_in,
    above,
    part_out,
    own_in,
    solved_out,
    solved_in,
    top_piece,
    gx_send,
    gx_recv,
    gy_send,
    gy_recv,
    gs_send,
    gs_recv,
    rhs_send,
    rhs_recv,
    row_send,
    row_recv,
    share_send,
    share_recv,
    up0_send,
    up0_recv,
    up_send,
    up_recv,
    down0_send,
    down0_recv,
    down_send,
    down_recv,
    own_send,
    own_recv,
    sample_send,
    sample_recv,
    solved_send,
    solved_recv,
    move_send,
    move_recv,
    top_send,
):
    rows = rhs_ref.shape[0]
    width = inv.shape[-1]
    slots = panel_ref.shape[0]
    tiles = pattern_ref.shape[2]
    tile = width // tiles
    span = NV * rows
    few = rhs_ref.shape[1] // NV
    f32, bf16 = jnp.float32, jnp.bfloat16
    root, top = nodes - 1, nodes // 2 - 1

    s = lax.axis_index("lvl")
    c = lax.axis_index("col")
    y, v = c // NV, c % NV
    x, core = v // 2, v % 2
    other = 1 - core

    level = 0
    step = 1
    for e in range(1, slots + 1):
        whole = 1 - ((s + 1) % 2**e + 2**e - 1) // 2**e
        level = level + whole
        step = step + whole * 2 ** (e - 1)
    side = (s // (2 * step)) % 2
    parent = (s + step * (1 - 2 * side)) % nodes
    left = (s + nodes - step // 2) % nodes
    right = (s + step // 2) % nodes
    one_root = (s + 1) // nodes
    one_top = (level + 1) // slots - one_root
    inner = s % 2
    is_root = one_root == 1
    is_top = one_top == 1
    not_root = one_root == 0
    is_leaf = inner == 0
    has_kids = inner * (1 - one_root) == 1
    has_parent = one_root + one_top == 0

    def chip(yy, xx, cc):
        return (yy * NX + xx) * 2 + cc

    own_span = pl.ds(pl.multiple_of(y * span, 128), span)

    barrier = pltpu.get_barrier_semaphore()

    def greet(lvl, col):
        pl.semaphore_signal(barrier, inc=1, device_id=(lvl, col), device_id_type=MESH)

    for d in range(1, NV):
        greet(s, y * NV + (v + d) % NV)
    for d in range(1, NY):
        greet(s, (y + d) % NY * NV + v)

    @pl.when(has_parent)
    def _():
        for w in range(NY):
            greet(parent, w * NV + v)

    @pl.when(has_kids)
    def _():
        for w in range(NY):
            greet(left, w * NV + v)
            greet(right, w * NV + v)

    @pl.when(is_top)
    def _():
        for q in range(NV):
            greet(root, y * NV + q)

    @pl.when(is_root)
    def _():
        for q in range(NV):
            greet(top, y * NV + q)

    inv[y, x, core] = inverse_ref[...]
    piece = 16

    def mask_slot(k):
        for q in range(rows // piece):
            tile_row = (c * rows + q * piece) // tile
            for j in range(tiles):
                keep = pattern_ref[k, tile_row, j].astype(f32)
                part = (slice(q * piece, (q + 1) * piece), slice(j * tile, (j + 1) * tile))
                block = panel_ref[(k,) + part]
                factor[(k, x, core) + part] = (block.astype(f32) * keep).astype(bf16)

    padded = jnp.concatenate(
        [rhs_ref[...], jnp.zeros((128 - rows, rhs_ref.shape[1]), f32)], axis=0
    )
    turned[...] = padded.T.reshape(NV, few, 128)
    rhs_in[v] = turned[v]
    mask_slot(0)

    pl.semaphore_wait(
        barrier,
        NV - 1
        + NY - 1
        + NY * (1 - one_root - one_top)
        + 2 * NY * inner * (1 - one_root)
        + NV * (one_top + one_root),
    )

    last = slots + 1

    def block(g, xx, cc):
        if g == 0:
            return inv.at[y, xx, cc]
        if g == last:
            return top_inv.at[xx, cc]
        return factor.at[g - 1, xx, cc]

    def gx_copy(g, i):
        if i == 0:
            ref, col = block(g, x, core), chip(y, x, other)
        elif i < NX:
            ref, col = block(g, x, core), chip(y, (x + i) % NX, core)
        else:
            ref, col = block(g, (x + 2 * NX - 1 - i) % NX, core), chip(y, x, other)
        return remote(ref, ref, gx_send.at[g, i], gx_recv.at[g, i], s, col)

    def gx_wait(g, i):
        if i == 0:
            ref = block(g, x, other)
        elif i < NX:
            ref = block(g, (x + NX - i) % NX, core)
        else:
            ref = block(g, (x + 2 * NX - 1 - i) % NX, other)
        arrived(ref, gx_recv.at[g, i])

    def gx_start(g):
        for i in ORDER + (0,):
            gx_copy(g, i).start()

    def gx_pass(g, then=None):
        for i in ORDER:
            gx_wait(g, i)
            gx_copy(g, i + NX - 1).start()
            if then is not None:
                then(i)

    def gx_finish(g):
        for i in (0,) + tuple(i + NX - 1 for i in ORDER):
            gx_wait(g, i)

    def each_y(body):
        for yy in range(NY):

            @pl.when(y == yy)
            def _(yy=yy):
                body(yy)

    def gy_copy(yy, d, j):
        ref = inv.at[yy, (x + j) % NX, core, :, yy * span :]
        col = chip((yy + d) % NY, x, core)
        return remote(ref, ref, gy_send.at[d, j], gy_recv.at[d, j], s, col)

    def gs_copy(yy, d):
        source = (yy + NY - d) % NY
        ref = inv.at[source, :, core, :, source * span :]
        return remote(ref, ref, gs_send.at[d], gs_recv.at[d], s, chip(yy, x, other))

    def gy_start(j):
        def body(yy):
            for d in ORDER:
                gy_copy(yy, d, j).start()

        each_y(body)

    def gy_pass():
        def body(yy):
            for d in ORDER:
                source = (yy + NY - d) % NY
                for j in range(NX):
                    arrived(
                        inv.at[source, (x + j) % NX, core, :, source * span :], gy_recv.at[d, j]
                    )
                gs_copy(yy, d).start()

        each_y(body)

    def gy_finish():
        def body(yy):
            for d in ORDER:
                source = (yy + NY - d) % NY
                arrived(inv.at[source, :, other, :, source * span :], gs_recv.at[d])

        each_y(body)

    def rhs_copy(d):
        to = (v + d) % NV
        return remote(turned.at[to], rhs_in.at[v], rhs_send.at[d], rhs_recv.at[d], s, y * NV + to)

    def row_copy(d):
        ref = rhs_all.at[:, own_span]
        return remote(ref, ref, row_send.at[d], row_recv.at[d], s, (y + d) % NY * NV + v)

    lane = lax.broadcasted_iota(jnp.int32, (few, 128), 1)

    def join_rhs():
        for d in range(1, NV):
            arrived(rhs_in.at[(v + NV - d) % NV], rhs_recv.at[d])
        joined = [jnp.zeros((few, 128), f32) for _ in range(span // 128)]
        for q in range(NV):
            a, b = divmod(q * rows, 128)
            moved = pltpu.roll(rhs_in[q], b, axis=1) if b else rhs_in[q]
            if b + rows <= 128:
                joined[a] = joined[a] + moved
            else:
                joined[a] = joined[a] + jnp.where(lane >= b, moved, 0.0)
                joined[a + 1] = joined[a + 1] + jnp.where(lane >= b, 0.0, moved)
        rhs_all[:, own_span] = jnp.concatenate(joined, axis=1)

    def share_copy(d):
        ref = shares.at[y]
        return remote(ref, ref, share_send.at[d], share_recv.at[d], s, (y + d) % NY * NV + v)

    def share_start(residual, rows_of):
        product = jnp.dot(residual, rows_of.reshape(span, width), preferred_element_type=f32)
        shares[y] = product.astype(bf16)
        for d in ORDER:
            share_copy(d).start()

    def share_sum():
        for d in ORDER:
            arrived(shares.at[(y + NY - d) % NY], share_recv.at[d])
        summed = shares[0].astype(f32)
        for w in range(1, NY):
            summed = summed + shares[w].astype(f32)
        return summed

    def up0_copy(w):
        return remote(
            push.at[0],
            first_in.at[side, :, own_span],
            up0_send.at[w],
            up0_recv.at[side, y],
            parent,
            w * NV + v,
        )

    def up_copy(k):
        return remote(
            push.at[k],
            later_in.at[side, k - 1],
            up_send.at[k],
            up_recv.at[side, k - 1],
            parent,
            y * NV + v,
        )

    def flat(k):
        return factor[k].reshape(span, width)

    def pushed(k, sample_half):
        return lax.dot_general(sample_half, flat(k), NT, preferred_element_type=f32)

    def cut_pieces(ref, value):
        parts = [value[:, 128 * a : 128 * (a + 1)] for a in range(span // 128)]
        for q in range(NV):
            a, b = divmod(q * rows, 128)
            moved = pltpu.roll(parts[a], 128 - b, axis=1) if b else parts[a]
            if b + rows > 128:
                after = pltpu.roll(parts[a + 1], 128 - b, axis=1)
                moved = jnp.where(lane < 128 - b, moved, after)
            ref[q] = moved

    def sample_copy(d):
        to = (v + d) % NV
        return remote(
            piece_out.at[to], sample_in.at[v], sample_send.at[d], sample_recv.at[d], s, y * NV + to
        )

    def solved_copy(d):
        to = (v + d) % NV
        return remote(
            solved_out.at[to], solved_in.at[v], solved_send.at[d], solved_recv.at[d], s, y * NV + to
        )

    def top_copy(i, d):
        to = (v + d) % NV
        ref, sem = (sample_in, sample_recv) if i == 0 else (solved_in, solved_recv)
        return remote(
            top_piece.at[i, to], ref.at[v], top_send.at[i, d], sem.at[d], root, y * NV + to
        )

    def sample_out():
        cut_pieces(piece_out, sample_t[:, own_span])
        sample_in[v] = piece_out[v]
        for d in range(1, NV):
            sample_copy(d).start()

    def move_inv():
        return remote(
            inverse_ref, top_inv.at[x, core], move_send.at[0], move_recv.at[0], top, c
        )

    def move_rhs():
        return remote(
            rhs_all.at[:, own_span], top_rhs, move_send.at[1], move_recv.at[1], top, c
        )

    def down_copy(k, child, i):
        return remote(
            above.at[k],
            above.at[k + 1],
            down_send.at[i, k],
            down_recv.at[k + 1],
            child,
            y * NV + v,
        )

    def down0_copy(w, child, i):
        return remote(
            part_out.at[w],
            parent_in.at[y],
            down0_send.at[i, w],
            down0_recv.at[y],
            child,
            w * NV + v,
        )

    def own_copy(d):
        to = (y + d) % NY
        return remote(part_out.at[to], own_in.at[y], own_send.at[d], own_recv.at[d], s, to * NV + v)

    def hand_down(k):
        @pl.when(has_kids)
        def _():
            down_copy(k, left, 0).start()
            down_copy(k, right, 1).start()

    @pl.when(is_leaf)
    def _():
        gx_start(0)
        for d in range(1, NV):
            rhs_copy(d).start()
        for k in range(1, slots):
            mask_slot(k)
        gx_pass(0, lambda i: gx_start(1) if i == ORDER[0] else None)
        join_rhs()
        gx_finish(0)
        share_start(rhs_all[:, own_span].astype(bf16), inv[y])
        gx_pass(1, lambda i: gx_start(2) if i == ORDER[0] and slots > 1 else None)
        sample_t[...] = share_sum()
        sample_half = sample_t[...].astype(bf16)
        for k in range(slots):
            if k > 0:
                gx_pass(
                    k + 1, lambda i: gx_start(k + 2) if i == ORDER[0] and k + 2 <= slots else None
                )
            gx_finish(k + 1)
            push[k] = pushed(k, sample_half).astype(bf16)
            if k == 0:
                for w in range(NY):
                    up0_copy(w).start()
            else:
                up_copy(k).start()
        for j in range(NX):
            gy_start(j)
        sample_out()
        gy_pass()
        gy_finish()

    @pl.when(inner == 1)
    def _():
        @pl.when(is_root)
        def _():
            move_inv().start()

        @pl.when(not_root)
        def _():
            gx_start(0)
            gy_start(0)

        for d in range(1, NV):
            rhs_copy(d).start()
        for k in range(1, slots - 1):
            mask_slot(k)

        @pl.when(not_root)
        def _():
            def follow(i):
                gy_start(NX - i)
                if i == ORDER[0]:
                    gx_start(1)

            gx_pass(0, follow)

        join_rhs()

        @pl.when(is_root)
        def _():
            move_rhs().start()

        @pl.when(not_root)
        def _():
            for d in range(1, NY):
                row_copy(d).start()
            gx_pass(1)
            for k in range(1, slots - 1):

                @pl.when(level + k < slots)
                def _():
                    gx_start(k + 1)

            @pl.when(is_top)
            def _():
                arrived(top_inv.at[x, core], move_recv.at[0])
                gx_start(last)

            for k in range(1, slots - 1):

                @pl.when(level + k < slots)
                def _():
                    gx_pass(k + 1)

            @pl.when(is_top)
            def _():
                gx_pass(last)

            gy_pass()
            for d in range(1, NY):
                group_of = (y + NY - d) % NY
                arrived(
                    rhs_all.at[:, pl.ds(pl.multiple_of(group_of * span, 128), span)],
                    row_recv.at[d],
                )
            gx_finish(0)
            gx_finish(1)
            for k in range(1, slots - 1):

                @pl.when(level + k < slots)
                def _():
                    gx_finish(k + 1)

            @pl.when(is_top)
            def _():
                gx_finish(last)
                arrived(top_rhs, move_recv.at[1])

            gy_finish()

            for i in range(2):
                for w in range(NY):
                    arrived(first_in.at[i, :, w * span : (w + 1) * span], up0_recv.at[i, w])
            incoming = first_in[0].astype(f32) + first_in[1].astype(f32)
            residual = (rhs_all[...] - incoming).astype(bf16)
            for w in range(NY):
                to = (w + 1) * span
                sample_t[:, w * span : to] = jnp.dot(
                    residual[:, :to],
                    inv[: w + 1, :, :, :, w * span : to].reshape(to, span),
                    preferred_element_type=f32,
                )
            sample_half = sample_t[...].astype(bf16)

            def pushed_sum(k):
                out = pushed(k, sample_half)
                for i in range(2):
                    arrived(later_in.at[i, k], up_recv.at[i, k])
                return out + later_in[0, k].astype(f32) + later_in[1, k].astype(f32)

            @pl.when(has_parent)
            def _():
                push[0] = pushed_sum(0).astype(bf16)
                for w in range(NY):
                    up0_copy(w).start()

            @pl.when(is_top)
            def _():
                residual_root = (top_rhs[...] - pushed_sum(0)).astype(bf16)
                share_start(residual_root, top_inv[...])
                root_t = share_sum()
                total[...] = root_t
                solved_root = lax.dot_general(
                    root_t.astype(bf16),
                    top_inv[...].reshape(span, width),
                    NT,
                    preferred_element_type=f32,
                )
                above[0] = solved_root.astype(bf16)
                down_copy(0, left, 0).start()
                down_copy(0, right, 1).start()
                cut_pieces(top_piece.at[1], solved_root)

            for k in range(1, slots - 1):

                @pl.when(level + k < slots)
                def _():
                    push[k] = pushed_sum(k).astype(bf16)
                    up_copy(k).start()

            @pl.when(level + 1 < slots)
            def _():
                sample_out()

    @pl.when(not_root)
    def _():
        group = lax.broadcasted_iota(jnp.int32, (few, width), 1) // span

        @pl.when(is_top)
        def _():
            cut_pieces(top_piece.at[0], total[:, own_span])

        total[...] = jnp.where(group == y, sample_t[...], 0.0)
        for k in range(slots - 1, 0, -1):

            @pl.when(level + k < slots)
            def _():
                arrived(above.at[k], down_recv.at[k])
                if k < slots - 1:
                    hand_down(k)
                total[...] -= jnp.dot(above[k], flat(k), preferred_element_type=f32)

        @pl.when(has_parent)
        def _():
            for w in range(NY):
                arrived(parent_in.at[w], down0_recv.at[w])
            summed = parent_in[0].astype(f32)
            for w in range(1, NY):
                summed = summed + parent_in[w].astype(f32)
            above[0] = summed.astype(bf16)

        total[...] -= jnp.dot(above[0], flat(0), preferred_element_type=f32)

        back = total[...].astype(bf16)
        for w in range(NY):
            start = w * span
            part = lax.dot_general(
                back[:, start:],
                inv[w, :, :, :, start:].reshape(span, width - start),
                NT,
                preferred_element_type=f32,
            )
            part_out[w] = part.astype(bf16)

            @pl.when(has_kids)
            def _():
                down0_copy(w, left, 0).start()
                down0_copy(w, right, 1).start()

        own_in[y] = part_out[y]
        for d in ORDER:
            own_copy(d).start()

        @pl.when(has_parent)
        def _():
            if slots > 1:
                hand_down(0)

        @pl.when(is_top)
        def _():
            for d in range(NV):
                top_copy(0, d).start()
                top_copy(1, d).start()
            sample_out()

        for d in range(1, NV):
            arrived(sample_in.at[(v + NV - d) % NV], sample_recv.at[d])
        sample_ref[...] = sample_in[...].reshape(NV * few, 128).T[:rows, :]

        for d in ORDER:
            arrived(own_in.at[(y + NY - d) % NY], own_recv.at[d])
        solved = own_in[0].astype(f32)
        for w in range(1, NY):
            solved = solved + own_in[w].astype(f32)
        cut_pieces(solved_out, solved)
        solved_in[v] = solved_out[v]
        for d in range(1, NV):
            solved_copy(d).start()
        for d in range(1, NV):
            arrived(solved_in.at[(v + NV - d) % NV], solved_recv.at[d])
        answer_ref[...] = solved_in[...].reshape(NV * few, 128).T[:rows, :]

    @pl.when(is_root)
    def _():
        for d in range(NV):
            arrived(sample_in.at[(v + NV - d) % NV], sample_recv.at[d])
            arrived(solved_in.at[(v + NV - d) % NV], solved_recv.at[d])
        sample_ref[...] = sample_in[...].reshape(NV * few, 128).T[:rows, :]
        answer_ref[...] = solved_in[...].reshape(NV * few, 128).T[:rows, :]

    for d in range(1, NV):
        rhs_copy(d).wait_send()

    def gx_sent(g):
        for i in range(2 * NX - 1):
            gx_copy(g, i).wait_send()

    @pl.when(is_root)
    def _():
        move_inv().wait_send()
        move_rhs().wait_send()

    @pl.when(not_root)
    def _():
        gx_sent(0)
        for k in range(slots):

            @pl.when(level + k < slots)
            def _():
                gx_sent(k + 1)

        def gy_sent(yy):
            for d in ORDER:
                for j in range(NX):
                    gy_copy(yy, d, j).wait_send()
                gs_copy(yy, d).wait_send()

        each_y(gy_sent)
        for d in range(1, NV):
            sample_copy(d).wait_send()
            solved_copy(d).wait_send()
        for d in ORDER:
            own_copy(d).wait_send()

    @pl.when(has_kids)
    def _():
        for d in range(1, NY):
            row_copy(d).wait_send()
        for i, child in enumerate((left, right)):
            for w in range(NY):
                down0_copy(w, child, i).wait_send()
            for k in range(slots - 1):

                @pl.when(level + k < slots)
                def _():
                    down_copy(k, child, i).wait_send()

    @pl.when(has_parent)
    def _():
        for w in range(NY):
            up0_copy(w).wait_send()
        for k in range(1, slots):

            @pl.when(level + k < slots)
            def _():
                up_copy(k).wait_send()

    def share_sent():
        for d in ORDER:
            share_copy(d).wait_send()

    @pl.when(is_leaf)
    def _():
        share_sent()

    @pl.when(is_top)
    def _():
        share_sent()
        gx_sent(last)
        for d in range(NV):
            top_copy(0, d).wait_send()
            top_copy(1, d).wait_send()


def on_device(nodes, rhs, panel, inverse_t, pattern):
    rows, count = rhs.shape[1:]
    slots = panel.shape[1]
    width = inverse_t.shape[2]
    span = NV * rows
    few = count // NV
    f32, bf16 = jnp.float32, jnp.bfloat16
    dma = pltpu.SemaphoreType.DMA
    vmem = pl.BlockSpec(memory_space=pltpu.VMEM)
    outs = pl.pallas_call(
        functools.partial(kernel, nodes),
        out_shape=[jax.ShapeDtypeStruct((rows, count), f32)] * 2,
        in_specs=[vmem, vmem, vmem, pl.BlockSpec(memory_space=pltpu.SMEM)],
        out_specs=[vmem, vmem],
        scratch_shapes=[
            pltpu.VMEM((slots, NX, 2, rows, width), bf16),
            pltpu.VMEM((NY, NX, 2, rows, width), bf16),
            pltpu.VMEM((NX, 2, rows, width), bf16),
            pltpu.VMEM((NV, few, 128), f32),
            pltpu.VMEM((NV, few, 128), f32),
            pltpu.VMEM((few, width), f32),
            pltpu.VMEM((few, span), f32),
            pltpu.VMEM((2, few, width), bf16),
            pltpu.VMEM((2, max(slots - 1, 1), few, span), bf16),
            pltpu.VMEM((slots, few, span), bf16),
            pltpu.VMEM((NY, few, width), bf16),
            pltpu.VMEM((few, width), f32),
            pltpu.VMEM((few, width), f32),
            pltpu.VMEM((NV, few, 128), f32),
            pltpu.VMEM((NV, few, 128), f32),
            pltpu.VMEM((NY, few, span), bf16),
            pltpu.VMEM((slots, few, span), bf16),
            pltpu.VMEM((NY, few, span), bf16),
            pltpu.VMEM((NY, few, span), bf16),
            pltpu.VMEM((NV, few, 128), f32),
            pltpu.VMEM((NV, few, 128), f32),
            pltpu.VMEM((2, NV, few, 128), f32),
        ]
        + [dma((slots + 2, 2 * NX - 1))] * 2
        + [dma((NY, NX))] * 2
        + [dma((NY,))] * 2
        + [dma((NV,))] * 2
        + [dma((NY,))] * 2
        + [dma((NY,))] * 2
        + [dma((NY,)), dma((2, NY))]
        + [dma((slots,)), dma((2, slots))]
        + [dma((2, NY)), dma((NY,))]
        + [dma((2, slots)), dma((slots,))]
        + [dma((NY,))] * 2
        + [dma((NV,))] * 4
        + [dma((2,))] * 2
        + [dma((2, NV))],
        compiler_params=pltpu.CompilerParams(
            collective_id=0, has_side_effects=True, vmem_limit_bytes=40 * 2**20
        ),
    )(rhs[0], panel[0], inverse_t[0], pattern[0])
    return outs[0][None], outs[1][None]


def solution(mesh):
    in_specs = (
        P("lvl", "col", None),
        P("lvl", None, "col", None),
        P("lvl", "col", None),
        P("lvl", None, None, None),
    )
    out_specs = (P("lvl", "col", None), P("lvl", "col", None))
    return jax.shard_map(
        functools.partial(on_device, mesh.shape["lvl"]),
        mesh=mesh,
        in_specs=in_specs,
        out_specs=out_specs,
        check_vma=False,
    )
```

time: 148 us -> 104 us (0.70)
  Pallas kernels: 143 us -> 99.1 us
    pallas_call x1, Pallas kernels: 143 us -> 99.1 us  [on_device(): pl.pallas_call(functools.partial(kernel, nodes), out_shape=[jax.ShapeDtyp...]
where the time goes in v2:
time: 104 us
  Pallas kernels  99.1 us (95%)
  local copies, waits for them, and re-layouts  3.94 us (4%)
    pallas_call x1, Pallas kernels, on_device(): pl.pallas_call(functools.partial(kernel, nodes), out_shape=[jax.ShapeDtyp...  99.1 us
    unnamed x9, local copies, waits for them, and re-layouts  3.94 us

profile of v2, /device:TPU:1, one launch (start us, length us, event | category | flops | bytes accessed | tf_op | source)
XLA Modules:
  0.0 103.7 jit_solution(9044235032816506757)
XLA Ops:
  0.6 0.0 copy-start.2
  0.6 0.7 copy.8
  1.4 0.0 copy-done.2
  1.4 0.0 copy-start
  1.4 1.1 %copy-done = bf16[1,4,48,1536]{3,2,1,0:T(8,128)(2,1)S(1)} copy-done((bf16[1,4,48,1536]{3,2,1,0:T(8,128)(2,1)S(1)}, bf16[1,4,48,1536]{3,2,1,0:T(8,128)(2,1)}, u32[]{:S(2)}) %copy-start) | copy-done | bytes 589848
  2.5 0.0 copy-start.1
  2.5 0.9 copy-done.1
  3.4 99.1 %shard_map.59 = (f32[48,128]{1,0:T(8,128)S(1)}, f32[48,128]{1,0:T(8,128)S(1)}) custom-call(f32[48,128]{1,0:T(8,128)S(1)} %bitcast.11, bf16[4,48,1536]{2,1,0:T(8,128)(2,1)S(1)} %bitcast.8, bf16[48,1536]{1,0:T(8,128)(2,1)S(1)} %bitcast.9, s32[4,12,12]{2,1,0:T(8,128)S(1)} %bitcast.10), custom_call_target="tpu_custom_call" | custom-call | tf_op jit(solution)/shard_map/pallas_call | solution.py:756
  102.4 0.6 copy.11
  103.1 0.6 copy.12
Async XLA Ops:
  0.6 0.8 copy-start.2
  1.4 1.1 %copy-start = (bf16[1,4,48,1536]{3,2,1,0:T(8,128)(2,1)S(1)}, bf16[1,4,48,1536]{3,2,1,0:T(8,128)(2,1)}, u32[]{:S(2)}) copy-start(bf16[1,4,48,1536]{3,2,1,0:T(8,128)(2,1)} %param.5) | copy-start | bytes 1769476
  2.5 0.9 copy-start.1

commit v3 on v2

--- a/solution.py
+++ b/solution.py
@@ -38,6 +38,9 @@
     pattern_ref,
     sample_ref,
     answer_ref,
+    rhs_own,
+    panel_own,
+    pattern_own,
     factor,
     inv,
     top_inv,
@@ -60,6 +63,8 @@
     solved_out,
     solved_in,
     top_piece,
+    root_sample,
+    root_solved,
     gx_send,
     gx_recv,
     gy_send,
@@ -89,6 +94,12 @@
     move_send,
     move_recv,
     top_send,
+    load_sem,
+    joint,
+    last_out,
+    last_in,
+    last_send,
+    last_recv,
 ):
     rows = rhs_ref.shape[0]
     width = inv.shape[-1]
@@ -136,10 +147,17 @@
     def greet(lvl, col):
         pl.semaphore_signal(barrier, inc=1, device_id=(lvl, col), device_id_type=MESH)
 
-    for d in range(1, NV):
-        greet(s, y * NV + (v + d) % NV)
-    for d in range(1, NY):
-        greet(s, (y + d) % NY * NV + v)
+    @pl.when(is_leaf)
+    def _():
+        for d in range(1, NY * NV):
+            greet(s, (c + d) % (NY * NV))
+
+    @pl.when(inner == 1)
+    def _():
+        for d in range(1, NV):
+            greet(s, y * NV + (v + d) % NV)
+        for d in range(1, NY):
+            greet(s, (y + d) % NY * NV + v)
 
     @pl.when(has_parent)
     def _():
@@ -162,29 +180,37 @@
         for q in range(NV):
             greet(top, y * NV + q)
 
-    inv[y, x, core] = inverse_ref[...]
+    loads = (
+        pltpu.make_async_copy(rhs_ref, rhs_own, load_sem.at[0]),
+        pltpu.make_async_copy(inverse_ref, inv.at[y, x, core], load_sem.at[1]),
+        pltpu.make_async_copy(pattern_ref, pattern_own, load_sem.at[2]),
+        pltpu.make_async_copy(panel_ref, panel_own, load_sem.at[3]),
+    )
+    for load in loads:
+        load.start()
     piece = 16
 
     def mask_slot(k):
         for q in range(rows // piece):
             tile_row = (c * rows + q * piece) // tile
             for j in range(tiles):
-                keep = pattern_ref[k, tile_row, j].astype(f32)
+                keep = pattern_own[k, tile_row, j].astype(f32)
                 part = (slice(q * piece, (q + 1) * piece), slice(j * tile, (j + 1) * tile))
-                block = panel_ref[(k,) + part]
+                block = panel_own[(k,) + part]
                 factor[(k, x, core) + part] = (block.astype(f32) * keep).astype(bf16)
 
+    loads[0].wait()
     padded = jnp.concatenate(
-        [rhs_ref[...], jnp.zeros((128 - rows, rhs_ref.shape[1]), f32)], axis=0
+        [rhs_own[...], jnp.zeros((128 - rows, rhs_ref.shape[1]), f32)], axis=0
     )
     turned[...] = padded.T.reshape(NV, few, 128)
     rhs_in[v] = turned[v]
-    mask_slot(0)
+    loads[1].wait()
 
     pl.semaphore_wait(
         barrier,
-        NV - 1
-        + NY - 1
+        (NV - 1 + NY - 1) * inner
+        + (NV * NY - 1) * (1 - inner)
         + NY * (1 - one_root - one_top)
         + 2 * NY * inner * (1 - one_root)
         + NV * (one_top + one_root),
@@ -226,7 +252,7 @@
             gx_wait(g, i)
             gx_copy(g, i + NX - 1).start()
             if then is not None:
-                then(i)
+                then(NX - i)
 
     def gx_finish(g):
         for i in (0,) + tuple(i + NX - 1 for i in ORDER):
@@ -352,7 +378,7 @@
             if b + rows > 128:
                 after = pltpu.roll(parts[a + 1], 128 - b, axis=1)
                 moved = jnp.where(lane < 128 - b, moved, after)
-            ref[q] = moved
+            ref[q] = moved.astype(ref.dtype)
 
     def sample_copy(d):
         to = (v + d) % NV
@@ -364,6 +390,17 @@
         to = (v + d) % NV
         return remote(
             solved_out.at[to], solved_in.at[v], solved_send.at[d], solved_recv.at[d], s, y * NV + to
+        )
+
+    def last_copy(d):
+        to = (c + d) % (NY * NV)
+        return remote(
+            last_out.at[to // NV, to % NV],
+            last_in.at[c],
+            last_send.at[d],
+            last_recv.at[d],
+            s,
+            to,
         )
 
     def top_copy(i, d):
@@ -381,7 +418,7 @@
 
     def move_inv():
         return remote(
-            inverse_ref, top_inv.at[x, core], move_send.at[0], move_recv.at[0], top, c
+            inv.at[y, x, core], top_inv.at[x, core], move_send.at[0], move_recv.at[0], top, c
         )
 
     def move_rhs():
@@ -419,24 +456,58 @@
             down_copy(k, left, 0).start()
             down_copy(k, right, 1).start()
 
+    def make_joint(k):
+        for w in range(NY):
+            start = w * span
+            joint[k, :, start : start + span] = lax.dot_general(
+                factor[k, :, :, :, start:].reshape(span, width - start),
+                inv[w, :, :, :, start:].reshape(span, width - start),
+                NT,
+                preferred_element_type=f32,
+            ).astype(bf16)
+
+    def make_base():
+        group = lax.broadcasted_iota(jnp.int32, (few, width), 1) // span
+        total[...] = jnp.where(group == y, sample_t[...], 0.0)
+        for k in range(slots - 1, 1, -1):
+
+            @pl.when(level + k < slots)
+            def _():
+                arrived(above.at[k], down_recv.at[k])
+                if k < slots - 1:
+                    hand_down(k)
+                total[...] -= jnp.dot(above[k], flat(k), preferred_element_type=f32)
+
+        back = total[...].astype(bf16)
+        for w in range(NY):
+            start = w * span
+            total[:, start : start + span] = lax.dot_general(
+                back[:, start:],
+                inv[w, :, :, :, start:].reshape(span, width - start),
+                NT,
+                preferred_element_type=f32,
+            )
+
     @pl.when(is_leaf)
     def _():
         gx_start(0)
         for d in range(1, NV):
             rhs_copy(d).start()
-        for k in range(1, slots):
+        loads[2].wait()
+        loads[3].wait()
+        for k in range(slots):
             mask_slot(k)
-        gx_pass(0, lambda i: gx_start(1) if i == ORDER[0] else None)
+        gx_pass(0, lambda j: gx_start(1) if j == 3 else None)
         join_rhs()
         gx_finish(0)
         share_start(rhs_all[:, own_span].astype(bf16), inv[y])
-        gx_pass(1, lambda i: gx_start(2) if i == ORDER[0] and slots > 1 else None)
+        gx_pass(1, lambda j: gx_start(2) if j == 3 and slots > 1 else None)
         sample_t[...] = share_sum()
         sample_half = sample_t[...].astype(bf16)
         for k in range(slots):
             if k > 0:
                 gx_pass(
-                    k + 1, lambda i: gx_start(k + 2) if i == ORDER[0] and k + 2 <= slots else None
+                    k + 1, lambda j: gx_start(k + 2) if j == 3 and k + 2 <= slots else None
                 )
             gx_finish(k + 1)
             push[k] = pushed(k, sample_half).astype(bf16)
@@ -450,6 +521,9 @@
         sample_out()
         gy_pass()
         gy_finish()
+        make_joint(0)
+        if slots > 1:
+            make_joint(1)
 
     @pl.when(inner == 1)
     def _():
@@ -464,14 +538,16 @@
 
         for d in range(1, NV):
             rhs_copy(d).start()
-        for k in range(1, slots - 1):
+        loads[2].wait()
+        loads[3].wait()
+        for k in range(max(slots - 1, 1)):
             mask_slot(k)
 
         @pl.when(not_root)
         def _():
-            def follow(i):
-                gy_start(NX - i)
-                if i == ORDER[0]:
+            def follow(j):
+                gy_start(j)
+                if j == 3:
                     gx_start(1)
 
             gx_pass(0, follow)
@@ -498,37 +574,23 @@
                 arrived(top_inv.at[x, core], move_recv.at[0])
                 gx_start(last)
 
-            for k in range(1, slots - 1):
-
-                @pl.when(level + k < slots)
-                def _():
-                    gx_pass(k + 1)
-
-            @pl.when(is_top)
-            def _():
-                gx_pass(last)
-
             gy_pass()
+            gx_finish(0)
+            gx_finish(1)
             for d in range(1, NY):
                 group_of = (y + NY - d) % NY
                 arrived(
                     rhs_all.at[:, pl.ds(pl.multiple_of(group_of * span, 128), span)],
                     row_recv.at[d],
                 )
-            gx_finish(0)
-            gx_finish(1)
-            for k in range(1, slots - 1):
-
-                @pl.when(level + k < slots)
-                def _():
-                    gx_finish(k + 1)
+            gy_finish()
 
             @pl.when(is_top)
             def _():
+                gx_pass(last)
                 gx_finish(last)
                 arrived(top_rhs, move_recv.at[1])
-
-            gy_finish()
+                make_joint(0)
 
             for i in range(2):
                 for w in range(NY):
@@ -560,86 +622,88 @@
             def _():
                 residual_root = (top_rhs[...] - pushed_sum(0)).astype(bf16)
                 share_start(residual_root, top_inv[...])
+                make_base()
                 root_t = share_sum()
-                total[...] = root_t
+                root_sample[...] = root_t
                 solved_root = lax.dot_general(
                     root_t.astype(bf16),
                     top_inv[...].reshape(span, width),
                     NT,
                     preferred_element_type=f32,
                 )
+                root_solved[...] = solved_root
                 above[0] = solved_root.astype(bf16)
                 down_copy(0, left, 0).start()
                 down_copy(0, right, 1).start()
-                cut_pieces(top_piece.at[1], solved_root)
 
             for k in range(1, slots - 1):
 
                 @pl.when(level + k < slots)
                 def _():
+                    gx_pass(k + 1)
+                    gx_finish(k + 1)
                     push[k] = pushed_sum(k).astype(bf16)
                     up_copy(k).start()
 
+            @pl.when(has_parent)
+            def _():
+                sample_out()
+                make_joint(0)
+                if slots > 1:
+                    make_joint(1)
+
+    @pl.when(not_root)
+    def _():
+        @pl.when(has_parent)
+        def _():
+            make_base()
+
             @pl.when(level + 1 < slots)
             def _():
-                sample_out()
-
-    @pl.when(not_root)
-    def _():
-        group = lax.broadcasted_iota(jnp.int32, (few, width), 1) // span
-
-        @pl.when(is_top)
-        def _():
-            cut_pieces(top_piece.at[0], total[:, own_span])
-
-        total[...] = jnp.where(group == y, sample_t[...], 0.0)
-        for k in range(slots - 1, 0, -1):
-
-            @pl.when(level + k < slots)
-            def _():
-                arrived(above.at[k], down_recv.at[k])
-                if k < slots - 1:
-                    hand_down(k)
-                total[...] -= jnp.dot(above[k], flat(k), preferred_element_type=f32)
-
-        @pl.when(has_parent)
-        def _():
+                arrived(above.at[1], down_recv.at[1])
+                hand_down(1)
+                total[...] -= jnp.dot(above[1], joint[1], preferred_element_type=f32)
+
             for w in range(NY):
                 arrived(parent_in.at[w], down0_recv.at[w])
             summed = parent_in[0].astype(f32)
             for w in range(1, NY):
                 summed = summed + parent_in[w].astype(f32)
             above[0] = summed.astype(bf16)
-
-        total[...] -= jnp.dot(above[0], flat(0), preferred_element_type=f32)
-
-        back = total[...].astype(bf16)
+            hand_down(0)
+
         for w in range(NY):
-            start = w * span
-            part = lax.dot_general(
-                back[:, start:],
-                inv[w, :, :, :, start:].reshape(span, width - start),
-                NT,
-                preferred_element_type=f32,
+            lanes = slice(w * span, (w + 1) * span)
+            part = total[:, lanes] - jnp.dot(
+                above[0], joint[0, :, lanes], preferred_element_type=f32
             )
             part_out[w] = part.astype(bf16)
 
+            @pl.when(is_leaf)
+            def _():
+                cut_pieces(last_out.at[w], part)
+
             @pl.when(has_kids)
             def _():
                 down0_copy(w, left, 0).start()
                 down0_copy(w, right, 1).start()
 
-        own_in[y] = part_out[y]
-        for d in ORDER:
-            own_copy(d).start()
-
-        @pl.when(has_parent)
-        def _():
-            if slots > 1:
-                hand_down(0)
+        @pl.when(is_leaf)
+        def _():
+            last_in[c] = last_out[y, v]
+            for d in range(1, NY * NV):
+                last_copy(d).start()
+
+        @pl.when(has_kids)
+        def _():
+            own_in[y] = part_out[y]
+            for d in ORDER:
+                own_copy(d).start()
 
         @pl.when(is_top)
         def _():
+            cut_pieces(top_piece.at[0], root_sample[:, own_span])
+            cut_pieces(top_piece.at[1], root_solved[...])
             for d in range(NV):
                 top_copy(0, d).start()
                 top_copy(1, d).start()
@@ -649,18 +713,30 @@
             arrived(sample_in.at[(v + NV - d) % NV], sample_recv.at[d])
         sample_ref[...] = sample_in[...].reshape(NV * few, 128).T[:rows, :]
 
-        for d in ORDER:
-            arrived(own_in.at[(y + NY - d) % NY], own_recv.at[d])
-        solved = own_in[0].astype(f32)
-        for w in range(1, NY):
-            solved = solved + own_in[w].astype(f32)
-        cut_pieces(solved_out, solved)
-        solved_in[v] = solved_out[v]
-        for d in range(1, NV):
-            solved_copy(d).start()
-        for d in range(1, NV):
-            arrived(solved_in.at[(v + NV - d) % NV], solved_recv.at[d])
-        answer_ref[...] = solved_in[...].reshape(NV * few, 128).T[:rows, :]
+        @pl.when(has_kids)
+        def _():
+            for d in ORDER:
+                arrived(own_in.at[(y + NY - d) % NY], own_recv.at[d])
+            solved = own_in[0].astype(f32)
+            for w in range(1, NY):
+                solved = solved + own_in[w].astype(f32)
+            cut_pieces(solved_out, solved)
+            solved_in[v] = solved_out[v]
+            for d in range(1, NV):
+                solved_copy(d).start()
+            for d in range(1, NV):
+                arrived(solved_in.at[(v + NV - d) % NV], solved_recv.at[d])
+            answer_ref[...] = solved_in[...].reshape(NV * few, 128).T[:rows, :]
+
+        @pl.when(is_leaf)
+        def _():
+            for d in range(1, NY * NV):
+                source = (c + NY * NV - d) % (NY * NV)
+                arrived(last_in.at[source], last_recv.at[d])
+            pieces = last_in[0:NV].astype(f32)
+            for w in range(1, NY):
+                pieces = pieces + last_in[w * NV : (w + 1) * NV].astype(f32)
+            answer_ref[...] = pieces.reshape(NV * few, 128).T[:rows, :]
 
     @pl.when(is_root)
     def _():
@@ -700,12 +776,13 @@
         each_y(gy_sent)
         for d in range(1, NV):
             sample_copy(d).wait_send()
+
+    @pl.when(has_kids)
+    def _():
+        for d in range(1, NV):
             solved_copy(d).wait_send()
         for d in ORDER:
             own_copy(d).wait_send()
-
-    @pl.when(has_kids)
-    def _():
         for d in range(1, NY):
             row_copy(d).wait_send()
         for i, child in enumerate((left, right)):
@@ -734,6 +811,8 @@
     @pl.when(is_leaf)
     def _():
         share_sent()
+        for d in range(1, NY * NV):
+            last_copy(d).wait_send()
 
     @pl.when(is_top)
     def _():
@@ -756,9 +835,12 @@
     outs = pl.pallas_call(
         functools.partial(kernel, nodes),
         out_shape=[jax.ShapeDtypeStruct((rows, count), f32)] * 2,
-        in_specs=[vmem, vmem, vmem, pl.BlockSpec(memory_space=pltpu.SMEM)],
+        in_specs=[pl.BlockSpec(memory_space=pltpu.HBM)] * 4,
         out_specs=[vmem, vmem],
         scratch_shapes=[
+            pltpu.VMEM((rows, count), f32),
+            pltpu.VMEM((slots, rows, width), bf16),
+            pltpu.SMEM(pattern.shape[1:], jnp.int32),
             pltpu.VMEM((slots, NX, 2, rows, width), bf16),
             pltpu.VMEM((NY, NX, 2, rows, width), bf16),
             pltpu.VMEM((NX, 2, rows, width), bf16),
@@ -781,6 +863,8 @@
             pltpu.VMEM((NV, few, 128), f32),
             pltpu.VMEM((NV, few, 128), f32),
             pltpu.VMEM((2, NV, few, 128), f32),
+            pltpu.VMEM((few, width), f32),
+            pltpu.VMEM((few, span), f32),
         ]
         + [dma((slots + 2, 2 * NX - 1))] * 2
         + [dma((NY, NX))] * 2
@@ -795,9 +879,12 @@
         + [dma((NY,))] * 2
         + [dma((NV,))] * 4
         + [dma((2,))] * 2
-        + [dma((2, NV))],
+        + [dma((2, NV))]
+        + [dma((4,)), pltpu.VMEM((2, span, width), bf16)]
+        + [pltpu.VMEM((NY, NV, few, 128), bf16), pltpu.VMEM((NY * NV, few, 128), bf16)]
+        + [dma((NY * NV,))] * 2,
         compiler_params=pltpu.CompilerParams(
-            collective_id=0, has_side_effects=True, vmem_limit_bytes=40 * 2**20
+            collective_id=0, has_side_effects=True, vmem_limit_bytes=56 * 2**20
         ),
     )(rhs[0], panel[0], inverse_t[0], pattern[0])
     return outs[0][None], outs[1][None]

time: 104 us -> 98.7 us (0.949)
  Pallas kernels: 99.1 us -> 94.5 us
    pallas_call x1, Pallas kernels: 99.1 us -> 94.5 us  [on_device(): pl.pallas_call(functools.partial(kernel, nodes), out_shape=[jax.ShapeDtyp...]
    unnamed x9 -> x5, local copies, waits for them, and re-layouts: 3.94 us -> 3.31 us
where the time goes in v3:
time: 98.7 us; the launch traced here: 98.4 us
  Pallas kernels  94.5 us (96%)
  local copies, waits for them, and re-layouts  3.31 us (3%)
    pallas_call x1, Pallas kernels, on_device(): pl.pallas_call(functools.partial(kernel, nodes), out_shape=[jax.ShapeDtyp...  94.5 us
    unnamed x5, local copies, waits for them, and re-layouts  3.31 us

profile of v3, /device:TPU:1, one launch (start us, length us, event | category | flops | bytes accessed | tf_op | source)
XLA Modules:
  0.0 98.4 jit_solution(12828585252915786597)
XLA Ops:
  0.6 1.3 %copy.8 = s32[1,4,12,12]{3,2,1,0:T(8,128)} copy(s32[1,4,12,12]{3,1,2,0:T(4,128)} %param.7) | data formatting | bytes 4608 | tf_op args[3]
  2.0 94.5 %shard_map.59 = (f32[48,128]{1,0:T(8,128)}, f32[48,128]{1,0:T(8,128)}) custom-call(f32[48,128]{1,0:T(8,128)} %bitcast.11, bf16[4,48,1536]{2,1,0:T(8,128)(2,1)} %bitcast.8, bf16[48,1536]{1,0:T(8,128)(2,1)} %bitcast.9, s32[4,12,12]{2,1,0:T(8,128)} %bitcast.10), custom_call_target="tpu_custom_call" | custom-call | tf_op jit(solution)/shard_map/pallas_call | solution.py:835
  96.5 0.0 copy-start
  96.5 1.4 %copy.11 = f32[1,48,128]{2,1,0:T(8,128)} copy(f32[1,48,128]{2,1,0:T(8,128)} %bitcast.13) | data formatting | bytes 49152
  97.8 0.0 copy-done
  97.8 0.6 copy.12
Async XLA Ops:
  96.5 1.4 %copy-start = (f32[48,128]{1,0:T(8,128)S(1)}, f32[48,128]{1,0:T(8,128)}, u32[]{:S(2)}) copy-start(f32[48,128]{1,0:T(8,128)} %get-tuple-element.5) | copy-start | bytes 73732

commit v4 on v3

--- a/solution.py
+++ b/solution.py
@@ -125,6 +125,12 @@
         step = step + whole * 2 ** (e - 1)
     side = (s // (2 * step)) % 2
     parent = (s + step * (1 - 2 * side)) % nodes
+    above_at = [parent]
+    for k in range(1, slots):
+        far = step * 2**k
+        above_at.append(
+            (above_at[-1] + far * (1 - 2 * ((above_at[-1] // (2 * far)) % 2)) + nodes) % nodes
+        )
     left = (s + nodes - step // 2) % nodes
     right = (s + step // 2) % nodes
     one_root = (s + 1) // nodes
@@ -180,6 +186,21 @@
         for q in range(NV):
             greet(top, y * NV + q)
 
+    def below(t):
+        return [i for i in range(2 ** (t + 1) - 1) if i != 2**t - 1]
+
+    for t in range(2, slots):
+
+        @pl.when(level == t)
+        def _(t=t):
+            for i in below(t):
+                if (i + 1) % 2 ** (t - 1):
+                    greet((s + nodes - 2**t + 1 + i) % nodes, c)
+
+    far_count = 0
+    for k in range(2, slots):
+        far_count = far_count + (slots - 1 - level + slots - k) // slots
+
     loads = (
         pltpu.make_async_copy(rhs_ref, rhs_own, load_sem.at[0]),
         pltpu.make_async_copy(inverse_ref, inv.at[y, x, core], load_sem.at[1]),
@@ -213,7 +234,8 @@
         + (NV * NY - 1) * (1 - inner)
         + NY * (1 - one_root - one_top)
         + 2 * NY * inner * (1 - one_root)
-        + NV * (one_top + one_root),
+        + NV * (one_top + one_root)
+        + far_count,
     )
 
     last = slots + 1
@@ -357,10 +379,10 @@
     def up_copy(k):
         return remote(
             push.at[k],
-            later_in.at[side, k - 1],
+            later_in.at[s % (step * 2 ** (k + 1))],
             up_send.at[k],
-            up_recv.at[side, k - 1],
-            parent,
+            up_recv.at[s % (step * 2 ** (k + 1))],
+            above_at[k - 1],
             y * NV + v,
         )
 
@@ -606,21 +628,24 @@
                 )
             sample_half = sample_t[...].astype(bf16)
 
-            def pushed_sum(k):
-                out = pushed(k, sample_half)
-                for i in range(2):
-                    arrived(later_in.at[i, k], up_recv.at[i, k])
-                return out + later_in[0, k].astype(f32) + later_in[1, k].astype(f32)
-
-            @pl.when(has_parent)
-            def _():
-                push[0] = pushed_sum(0).astype(bf16)
-                for w in range(NY):
-                    up0_copy(w).start()
+            def pushed_sum(t):
+                out = pushed(0, sample_half)
+                for i in below(t):
+                    arrived(later_in.at[i], up_recv.at[i])
+                    out = out + later_in[i].astype(f32)
+                return out
+
+            for t in range(1, slots - 1):
+
+                @pl.when(level == t)
+                def _(t=t):
+                    push[0] = pushed_sum(t).astype(bf16)
+                    for w in range(NY):
+                        up0_copy(w).start()
 
             @pl.when(is_top)
             def _():
-                residual_root = (top_rhs[...] - pushed_sum(0)).astype(bf16)
+                residual_root = (top_rhs[...] - pushed_sum(slots - 1)).astype(bf16)
                 share_start(residual_root, top_inv[...])
                 make_base()
                 root_t = share_sum()
@@ -642,7 +667,7 @@
                 def _():
                     gx_pass(k + 1)
                     gx_finish(k + 1)
-                    push[k] = pushed_sum(k).astype(bf16)
+                    push[k] = pushed(k, sample_half).astype(bf16)
                     up_copy(k).start()
 
             @pl.when(has_parent)
@@ -849,7 +874,7 @@
             pltpu.VMEM((few, width), f32),
             pltpu.VMEM((few, span), f32),
             pltpu.VMEM((2, few, width), bf16),
-            pltpu.VMEM((2, max(slots - 1, 1), few, span), bf16),
+            pltpu.VMEM((2**slots - 1, few, span), bf16),
             pltpu.VMEM((slots, few, span), bf16),
             pltpu.VMEM((NY, few, width), bf16),
             pltpu.VMEM((few, width), f32),
@@ -873,7 +898,7 @@
         + [dma((NY,))] * 2
         + [dma((NY,))] * 2
         + [dma((NY,)), dma((2, NY))]
-        + [dma((slots,)), dma((2, slots))]
+        + [dma((slots,)), dma((2**slots - 1,))]
         + [dma((2, NY)), dma((NY,))]
         + [dma((2, slots)), dma((slots,))]
         + [dma((NY,))] * 2

time: 98.7 us -> 100 us (1.013)
  Pallas kernels: 94.5 us -> 96.1 us
    pallas_call x1, Pallas kernels: 94.5 us -> 96.1 us  [on_device(): pl.pallas_call(functools.partial(kernel, nodes), out_shape=[jax.ShapeDtyp...]
where the time goes in v4:
time: 100 us
  Pallas kernels  96.1 us (96%)
  local copies, waits for them, and re-layouts  3.31 us (3%)
    pallas_call x1, Pallas kernels, on_device(): pl.pallas_call(functools.partial(kernel, nodes), out_shape=[jax.ShapeDtyp...  96.1 us
    unnamed x5, local copies, waits for them, and re-layouts  3.31 us

profile of v4, /device:TPU:1, one launch (start us, length us, event | category | flops | bytes accessed | tf_op | source)
XLA Modules:
  0.0 100.0 jit_solution(6184688733617594284)
XLA Ops:
  0.6 1.3 %copy.8 = s32[1,4,12,12]{3,2,1,0:T(8,128)} copy(s32[1,4,12,12]{3,1,2,0:T(4,128)} %param.7) | data formatting | bytes 4608 | tf_op args[3]
  2.0 96.1 %shard_map.59 = (f32[48,128]{1,0:T(8,128)}, f32[48,128]{1,0:T(8,128)}) custom-call(f32[48,128]{1,0:T(8,128)} %bitcast.11, bf16[4,48,1536]{2,1,0:T(8,128)(2,1)} %bitcast.8, bf16[48,1536]{1,0:T(8,128)(2,1)} %bitcast.9, s32[4,12,12]{2,1,0:T(8,128)} %bitcast.10), custom_call_target="tpu_custom_call" | custom-call | tf_op jit(solution)/shard_map/pallas_call | solution.py:860
  98.0 0.0 copy-start
  98.1 1.4 %copy.11 = f32[1,48,128]{2,1,0:T(8,128)} copy(f32[1,48,128]{2,1,0:T(8,128)} %bitcast.13) | data formatting | bytes 49152
  99.4 0.0 copy-done
  99.4 0.6 copy.12
Async XLA Ops:
  98.0 1.4 %copy-start = (f32[48,128]{1,0:T(8,128)S(1)}, f32[48,128]{1,0:T(8,128)}, u32[]{:S(2)}) copy-start(f32[48,128]{1,0:T(8,128)} %get-tuple-element.5) | copy-start | bytes 73732

commit v5 on v4

--- a/solution.py
+++ b/solution.py
@@ -376,6 +376,16 @@
             w * NV + v,
         )
 
+    def leaf_copy():
+        return remote(
+            push.at[0],
+            first_in.at[side, :, own_span],
+            up0_send.at[0],
+            up0_recv.at[side, y],
+            parent,
+            c,
+        )
+
     def up_copy(k):
         return remote(
             push.at[k],
@@ -519,23 +529,24 @@
         loads[3].wait()
         for k in range(slots):
             mask_slot(k)
-        gx_pass(0, lambda j: gx_start(1) if j == 3 else None)
+            if k == 0:
+                gx_start(1)
+        gx_pass(0, lambda j: gx_start(2) if j == 3 and slots > 1 else None)
         join_rhs()
         gx_finish(0)
         share_start(rhs_all[:, own_span].astype(bf16), inv[y])
-        gx_pass(1, lambda j: gx_start(2) if j == 3 and slots > 1 else None)
+        gx_pass(1, lambda j: gx_start(3) if j == 3 and slots > 2 else None)
         sample_t[...] = share_sum()
         sample_half = sample_t[...].astype(bf16)
         for k in range(slots):
             if k > 0:
                 gx_pass(
-                    k + 1, lambda j: gx_start(k + 2) if j == 3 and k + 2 <= slots else None
+                    k + 1, lambda j: gx_start(k + 3) if j == 3 and k + 3 <= slots else None
                 )
             gx_finish(k + 1)
             push[k] = pushed(k, sample_half).astype(bf16)
             if k == 0:
-                for w in range(NY):
-                    up0_copy(w).start()
+                leaf_copy().start()
             else:
                 up_copy(k).start()
         for j in range(NX):
@@ -596,36 +607,54 @@
                 arrived(top_inv.at[x, core], move_recv.at[0])
                 gx_start(last)
 
-            gy_pass()
-            gx_finish(0)
-            gx_finish(1)
-            for d in range(1, NY):
-                group_of = (y + NY - d) % NY
-                arrived(
-                    rhs_all.at[:, pl.ds(pl.multiple_of(group_of * span, 128), span)],
-                    row_recv.at[d],
-                )
-            gy_finish()
-
-            @pl.when(is_top)
-            def _():
-                gx_pass(last)
-                gx_finish(last)
-                arrived(top_rhs, move_recv.at[1])
-                make_joint(0)
-
-            for i in range(2):
+            def rest_of_inverse():
+                gy_pass()
+                for d in range(1, NY):
+                    group_of = (y + NY - d) % NY
+                    arrived(
+                        rhs_all.at[:, pl.ds(pl.multiple_of(group_of * span, 128), span)],
+                        row_recv.at[d],
+                    )
+                gy_finish()
+
+            @pl.when(level == 1)
+            def _():
+                gx_finish(0)
+                for i in range(2):
+                    arrived(first_in.at[i, :, own_span], up0_recv.at[i, y])
+                incoming = first_in[0, :, own_span].astype(f32) + first_in[
+                    1, :, own_span
+                ].astype(f32)
+                share_start((rhs_all[:, own_span] - incoming).astype(bf16), inv[y])
+                gx_finish(1)
+                sample_t[...] = share_sum()
+
+            @pl.when(level > 1)
+            def _():
+                rest_of_inverse()
+                gx_finish(0)
+                gx_finish(1)
+
+                @pl.when(is_top)
+                def _():
+                    gx_pass(last)
+                    gx_finish(last)
+                    arrived(top_rhs, move_recv.at[1])
+                    make_joint(0)
+
+                for i in range(2):
+                    for w in range(NY):
+                        arrived(first_in.at[i, :, w * span : (w + 1) * span], up0_recv.at[i, w])
+                incoming = first_in[0].astype(f32) + first_in[1].astype(f32)
+                residual = (rhs_all[...] - incoming).astype(bf16)
                 for w in range(NY):
-                    arrived(first_in.at[i, :, w * span : (w + 1) * span], up0_recv.at[i, w])
-            incoming = first_in[0].astype(f32) + first_in[1].astype(f32)
-            residual = (rhs_all[...] - incoming).astype(bf16)
-            for w in range(NY):
-                to = (w + 1) * span
-                sample_t[:, w * span : to] = jnp.dot(
-                    residual[:, :to],
-                    inv[: w + 1, :, :, :, w * span : to].reshape(to, span),
-                    preferred_element_type=f32,
-                )
+                    to = (w + 1) * span
+                    sample_t[:, w * span : to] = jnp.dot(
+                        residual[:, :to],
+                        inv[: w + 1, :, :, :, w * span : to].reshape(to, span),
+                        preferred_element_type=f32,
+                    )
+
             sample_half = sample_t[...].astype(bf16)
 
             def pushed_sum(t):
@@ -673,6 +702,11 @@
             @pl.when(has_parent)
             def _():
                 sample_out()
+
+                @pl.when(level == 1)
+                def _():
+                    rest_of_inverse()
+
                 make_joint(0)
                 if slots > 1:
                     make_joint(1)
@@ -821,8 +855,11 @@
 
     @pl.when(has_parent)
     def _():
-        for w in range(NY):
-            up0_copy(w).wait_send()
+        @pl.when(inner == 1)
+        def _():
+            for w in range(NY):
+                up0_copy(w).wait_send()
+
         for k in range(1, slots):
 
             @pl.when(level + k < slots)
@@ -836,8 +873,13 @@
     @pl.when(is_leaf)
     def _():
         share_sent()
+        leaf_copy().wait_send()
         for d in range(1, NY * NV):
             last_copy(d).wait_send()
+
+    @pl.when(level == 1)
+    def _():
+        share_sent()
 
     @pl.when(is_top)
     def _():

time: 100 us -> 98.4 us (0.984)
  Pallas kernels: 96.1 us -> 94.2 us
    pallas_call x1, Pallas kernels: 96.1 us -> 94.2 us  [on_device(): pl.pallas_call(functools.partial(kernel, nodes), out_shape=[jax.ShapeDtyp...]
where the time goes in v5:
time: 98.4 us; the launch traced here: 98.2 us
  Pallas kernels  94.2 us (96%)
  local copies, waits for them, and re-layouts  3.31 us (3%)
    pallas_call x1, Pallas kernels, on_device(): pl.pallas_call(functools.partial(kernel, nodes), out_shape=[jax.ShapeDtyp...  94.2 us
    unnamed x5, local copies, waits for them, and re-layouts  3.31 us

profile of v5, /device:TPU:1, one launch (start us, length us, event | category | flops | bytes accessed | tf_op | source)
XLA Modules:
  0.0 98.2 jit_solution(17656523722975076851)
XLA Ops:
  0.6 1.3 %copy.8 = s32[1,4,12,12]{3,2,1,0:T(8,128)} copy(s32[1,4,12,12]{3,1,2,0:T(4,128)} %param.7) | data formatting | bytes 4608 | tf_op args[3]
  2.0 94.2 %shard_map.59 = (f32[48,128]{1,0:T(8,128)}, f32[48,128]{1,0:T(8,128)}) custom-call(f32[48,128]{1,0:T(8,128)} %bitcast.11, bf16[4,48,1536]{2,1,0:T(8,128)(2,1)} %bitcast.8, bf16[48,1536]{1,0:T(8,128)(2,1)} %bitcast.9, s32[4,12,12]{2,1,0:T(8,128)} %bitcast.10), custom_call_target="tpu_custom_call" | custom-call | tf_op jit(solution)/shard_map/pallas_call | solution.py:902
  96.2 0.0 copy-start
  96.2 1.4 %copy.11 = f32[1,48,128]{2,1,0:T(8,128)} copy(f32[1,48,128]{2,1,0:T(8,128)} %bitcast.13) | data formatting | bytes 49152
  97.6 0.0 copy-done
  97.6 0.6 copy.12
Async XLA Ops:
  96.2 1.4 %copy-start = (f32[48,128]{1,0:T(8,128)S(1)}, f32[48,128]{1,0:T(8,128)}, u32[]{:S(2)}) copy-start(f32[48,128]{1,0:T(8,128)} %get-tuple-element.5) | copy-start | bytes 73732

commit v6 on v5

--- a/solution.py
+++ b/solution.py
@@ -332,6 +332,13 @@
         ref = rhs_all.at[:, own_span]
         return remote(ref, ref, row_send.at[d], row_recv.at[d], s, (y + d) % NY * NV + v)
 
+    def rows_arrived():
+        for d in range(1, NY):
+            group_of = (y + NY - d) % NY
+            arrived(
+                rhs_all.at[:, pl.ds(pl.multiple_of(group_of * span, 128), span)], row_recv.at[d]
+            )
+
     lane = lax.broadcasted_iota(jnp.int32, (few, 128), 1)
 
     def join_rhs():
@@ -489,14 +496,19 @@
             down_copy(k, right, 1).start()
 
     def make_joint(k):
-        for w in range(NY):
-            start = w * span
-            joint[k, :, start : start + span] = lax.dot_general(
-                factor[k, :, :, :, start:].reshape(span, width - start),
-                inv[w, :, :, :, start:].reshape(span, width - start),
-                NT,
-                preferred_element_type=f32,
-            ).astype(bf16)
+        def some_rows(r, carry):
+            at = pl.ds(pl.multiple_of(r * 2 * rows, 2 * rows), 2 * rows)
+            for w in range(NY):
+                start = w * span
+                joint[k, at, start : start + span] = lax.dot_general(
+                    factor[k, r, :, :, start:].reshape(2 * rows, width - start),
+                    inv[w, :, :, :, start:].reshape(span, width - start),
+                    NT,
+                    preferred_element_type=f32,
+                ).astype(bf16)
+            return carry
+
+        lax.fori_loop(0, NX, some_rows, 0)
 
     def make_base():
         group = lax.broadcasted_iota(jnp.int32, (few, width), 1) // span
@@ -547,16 +559,10 @@
             push[k] = pushed(k, sample_half).astype(bf16)
             if k == 0:
                 leaf_copy().start()
+                for j in range(NX):
+                    gy_start(j)
             else:
                 up_copy(k).start()
-        for j in range(NX):
-            gy_start(j)
-        sample_out()
-        gy_pass()
-        gy_finish()
-        make_joint(0)
-        if slots > 1:
-            make_joint(1)
 
     @pl.when(inner == 1)
     def _():
@@ -606,16 +612,6 @@
             def _():
                 arrived(top_inv.at[x, core], move_recv.at[0])
                 gx_start(last)
-
-            def rest_of_inverse():
-                gy_pass()
-                for d in range(1, NY):
-                    group_of = (y + NY - d) % NY
-                    arrived(
-                        rhs_all.at[:, pl.ds(pl.multiple_of(group_of * span, 128), span)],
-                        row_recv.at[d],
-                    )
-                gy_finish()
 
             @pl.when(level == 1)
             def _():
@@ -631,7 +627,9 @@
 
             @pl.when(level > 1)
             def _():
-                rest_of_inverse()
+                gy_pass()
+                rows_arrived()
+                gy_finish()
                 gx_finish(0)
                 gx_finish(1)
 
@@ -699,17 +697,25 @@
                     push[k] = pushed(k, sample_half).astype(bf16)
                     up_copy(k).start()
 
-            @pl.when(has_parent)
-            def _():
-                sample_out()
-
-                @pl.when(level == 1)
-                def _():
-                    rest_of_inverse()
-
-                make_joint(0)
-                if slots > 1:
-                    make_joint(1)
+    @pl.when(has_parent)
+    def _():
+        sample_out()
+
+        @pl.when(level < 2)
+        def _():
+            gy_pass()
+
+            @pl.when(level == 1)
+            def _():
+                rows_arrived()
+
+            gy_finish()
+
+        def one_joint(k, carry):
+            make_joint(k)
+            return carry
+
+        lax.fori_loop(0, min(slots, 2), one_joint, 0)
 
     @pl.when(not_root)
     def _():

time: 98.4 us -> 96.2 us (0.978)
  Pallas kernels: 94.2 us -> 92 us
    pallas_call x1, Pallas kernels: 94.2 us -> 92 us  [on_device(): pl.pallas_call(functools.partial(kernel, nodes), out_shape=[jax.ShapeDtyp...]
where the time goes in v6:
time: 96.2 us; the launch traced here: 96 us
  Pallas kernels  92 us (96%)
  local copies, waits for them, and re-layouts  3.31 us (3%)
    pallas_call x1, Pallas kernels, on_device(): pl.pallas_call(functools.partial(kernel, nodes), out_shape=[jax.ShapeDtyp...  92 us
    unnamed x5, local copies, waits for them, and re-layouts  3.31 us

profile of v6, /device:TPU:1, one launch (start us, length us, event | category | flops | bytes accessed | tf_op | source)
XLA Modules:
  0.0 96.0 jit_solution(5642090762014963205)
XLA Ops:
  0.6 1.3 %copy.8 = s32[1,4,12,12]{3,2,1,0:T(8,128)} copy(s32[1,4,12,12]{3,1,2,0:T(4,128)} %param.7) | data formatting | bytes 4608 | tf_op args[3]
  2.0 92.0 %shard_map.59 = (f32[48,128]{1,0:T(8,128)}, f32[48,128]{1,0:T(8,128)}) custom-call(f32[48,128]{1,0:T(8,128)} %bitcast.11, bf16[4,48,1536]{2,1,0:T(8,128)(2,1)} %bitcast.8, bf16[48,1536]{1,0:T(8,128)(2,1)} %bitcast.9, s32[4,12,12]{2,1,0:T(8,128)} %bitcast.10), custom_call_target="tpu_custom_call" | custom-call | tf_op jit(solution)/shard_map/pallas_call | solution.py:908
  94.0 0.0 copy-start
  94.0 1.4 %copy.11 = f32[1,48,128]{2,1,0:T(8,128)} copy(f32[1,48,128]{2,1,0:T(8,128)} %bitcast.13) | data formatting | bytes 49152
  95.4 0.0 copy-done
  95.4 0.6 copy.12
Async XLA Ops:
  94.0 1.4 %copy-start = (f32[48,128]{1,0:T(8,128)S(1)}, f32[48,128]{1,0:T(8,128)}, u32[]{:S(2)}) copy-start(f32[48,128]{1,0:T(8,128)} %get-tuple-element.5) | copy-start | bytes 73732

commit v7 on v6

--- a/solution.py
+++ b/solution.py
@@ -543,10 +543,12 @@
             mask_slot(k)
             if k == 0:
                 gx_start(1)
-        gx_pass(0, lambda j: gx_start(2) if j == 3 and slots > 1 else None)
+        gx_pass(0)
         join_rhs()
         gx_finish(0)
         share_start(rhs_all[:, own_span].astype(bf16), inv[y])
+        if slots > 1:
+            gx_start(2)
         gx_pass(1, lambda j: gx_start(3) if j == 3 and slots > 2 else None)
         sample_t[...] = share_sum()
         sample_half = sample_t[...].astype(bf16)

time: 96.2 us -> 96.2 us (level)
  no operation moved by 1% of the time
where the time goes in v7:
time: 96.2 us; the launch traced here: 96 us
  Pallas kernels  92 us (96%)
  local copies, waits for them, and re-layouts  3.31 us (3%)
    pallas_call x1, Pallas kernels, on_device(): pl.pallas_call(functools.partial(kernel, nodes), out_shape=[jax.ShapeDtyp...  92 us
    unnamed x5, local copies, waits for them, and re-layouts  3.31 us

profile of v7, /device:TPU:1, one launch (start us, length us, event | category | flops | bytes accessed | tf_op | source)
XLA Modules:
  0.0 96.0 jit_solution(12645664580633338845)
XLA Ops:
  0.6 1.3 %copy.8 = s32[1,4,12,12]{3,2,1,0:T(8,128)} copy(s32[1,4,12,12]{3,1,2,0:T(4,128)} %param.7) | data formatting | bytes 4608 | tf_op args[3]
  2.0 92.0 %shard_map.59 = (f32[48,128]{1,0:T(8,128)}, f32[48,128]{1,0:T(8,128)}) custom-call(f32[48,128]{1,0:T(8,128)} %bitcast.11, bf16[4,48,1536]{2,1,0:T(8,128)(2,1)} %bitcast.8, bf16[48,1536]{1,0:T(8,128)(2,1)} %bitcast.9, s32[4,12,12]{2,1,0:T(8,128)} %bitcast.10), custom_call_target="tpu_custom_call" | custom-call | tf_op jit(solution)/shard_map/pallas_call | solution.py:910
  94.0 0.0 copy-start
  94.0 1.4 %copy.11 = f32[1,48,128]{2,1,0:T(8,128)} copy(f32[1,48,128]{2,1,0:T(8,128)} %bitcast.13) | data formatting | bytes 49152
  95.4 0.0 copy-done
  95.4 0.6 copy.12
Async XLA Ops:
  94.0 1.4 %copy-start = (f32[48,128]{1,0:T(8,128)S(1)}, f32[48,128]{1,0:T(8,128)}, u32[]{:S(2)}) copy-start(f32[48,128]{1,0:T(8,128)} %get-tuple-element.5) | copy-start | bytes 73732
